TPU v7x, 32 devices: a whole 2x2x4 slice. The times are simulated.
32 devices in a mesh: band: 8 (over z, y), chan: 4 (over x, core).
Axes of the slice: x: 2, y: 2, z: 4, core: 2. Of those that a mesh axis runs over, the one named last changes fastest.
Arguments:
- spectra: bfloat16 [2, 2, 16384, 64], P(None, None, 'chan', 'band')
- window_flags: int32 [2, 128], replicated, may hold values 0 or 1
- pair_tiles: int32 [4, 8, 2], P('chan'), may hold values from 0 to 127, as said below
- owners: int32 [4, 8, 1], P('chan'), may hold values from 0 to 7; in each aligned block of 8 rows (0 to 7, 8 to 15, ..., all dimensions but the last counted through in order) at most 2 rows name the same one
- stacks: float32 [4, 16, 512, 128], P('chan', 'band'), may hold values from -3 to 3
Outputs:
- new_stacks: float32 [4, 16, 512, 128], P('chan', 'band')
Inputs may be any that keep to these rules, and one draw needn't show every extreme that they name: `pair_tiles`: entry 0 is a tile of the pair's own quarter q (q * 32 to q * 32 + 31) and entry 1 = entry 0 + d: either 0 <= d <= 7, with d even where entry 1 lies in the quarter above, or -7 <= d < 0 with entry 1 in the quarter below and d odd. No two pair tiles of the whole cable join the same two tiles. Every quarter has a pair with d = 7, and every quarter but the first one with d = -7. `owners`: no owner holds more than 2 pair tiles of one quarter; some owner holds exactly 2.
All inputs are finite; a program needn't handle non-finite values.
Results may differ from a plain program's by a relative error of at most 0.0039.
Values may be sent and summed in bfloat16 or wider, within the bound.
No kernel may reach another device: no remote copies, remote signals or barrier semaphores. Data moves between devices by JAX's collectives and lax.ppermute only.
A program may use at most 64 MiB of HBM per device.

v0:
```python
import math

import jax
import jax.numpy as jnp
from jax import lax
from jax.sharding import PartitionSpec as P

TILE = 128
MAXOFF = 7
LAGS = 512
CAP = 2


STABILITY_FLOOR = 1e-05


def padded(shard, sides, width):
    for axis, dim in sides:
        size, length = (lax.axis_size(axis), shard.shape[dim])
        up = [(i, (i + 1) % size) for i in range(size - 1)]
        down = [(j, i) for i, j in up]
        last = lax.slice_in_dim(shard, length - width, length, axis=dim)
        first = lax.slice_in_dim(shard, 0, width, axis=dim)
        before = lax.ppermute(last, axis, up)
        after = lax.ppermute(first, axis, down)
        shard = jnp.concatenate([before, shard, after], axis=dim)
    return shard


def lag_table(first_bin, bin_count, total_bins):
    frequency = first_bin + lax.iota(jnp.int32, bin_count)
    lag_shift = lax.iota(jnp.int32, LAGS) - LAGS // 2
    phase_index = jnp.mod(lag_shift[:, None] * frequency[None, :], total_bins)
    angles = phase_index.astype(jnp.float32) * (2.0 * math.pi / total_bins)
    amplitude = 1.0 / math.sqrt(total_bins)
    return jnp.concatenate(
        [jnp.cos(angles) * amplitude, -jnp.sin(angles) * amplitude], axis=1
    ).astype(jnp.bfloat16)


def whiten(spectra, window_flags, quarter):
    tiles_here = spectra.shape[2] // TILE
    values = spectra.astype(jnp.float32)
    energy = values[:, 0] * values[:, 0] + values[:, 1] * values[:, 1]
    level = jnp.sqrt(jnp.mean(energy, axis=-1) + STABILITY_FLOOR)
    tile_validity_flags = lax.dynamic_slice_in_dim(
        window_flags, quarter * tiles_here, tiles_here, 1
    ).astype(jnp.float32)
    gate = jnp.repeat(tile_validity_flags, TILE, axis=1)
    return (values / level[:, None, :, None] * gate[:, None, :, None]).astype(jnp.bfloat16)


def block_cross(left_tiles, right_tiles, divisor):
    left_real = left_tiles[:, 0].astype(jnp.float32)
    left_imag = left_tiles[:, 1].astype(jnp.float32)
    right_real = right_tiles[:, 0].astype(jnp.float32)
    right_imag = right_tiles[:, 1].astype(jnp.float32)
    real_part = jnp.sum(left_real * right_real + left_imag * right_imag, axis=0)
    imaginary_component = jnp.sum(left_real * right_imag - left_imag * right_real, axis=0)
    return (
        jnp.concatenate([real_part, imaginary_component], axis=-1) / divisor[:, None, None]
    ).astype(jnp.bfloat16)


def body(spectra, window_flags, pair_tiles, owners, stacks):
    quarter = lax.axis_index("chan")
    band_size = lax.axis_size("band")
    bin_count = spectra.shape[3]
    tiles_here = spectra.shape[2] // TILE
    whitened = whiten(spectra, window_flags, quarter)
    extended = padded(whitened, (("chan", 2),), MAXOFF * TILE)
    offset = quarter * tiles_here - MAXOFF
    tile_blocks = extended.reshape(extended.shape[0], 2, extended.shape[2] // TILE, TILE, bin_count)
    pair_list = pair_tiles[0]
    owner_ids = owners[0, :, 0]
    count_pairs = pair_list.shape[0]
    source = pair_list[:, 0]
    target = pair_list[:, 1]
    flags_real = window_flags.astype(jnp.float32)
    columns = lax.iota(jnp.int32, window_flags.shape[1])
    pick_source = (source[:, None] == columns[None, :]).astype(jnp.float32)
    pick_target = (target[:, None] == columns[None, :]).astype(jnp.float32)
    source_flags = jnp.dot(pick_source, flags_real.T, precision=lax.Precision.HIGHEST)
    target_flags = jnp.dot(pick_target, flags_real.T, precision=lax.Precision.HIGHEST)
    divisor = jnp.maximum(jnp.sum(source_flags * target_flags, axis=1), 1.0)
    local_source = source - offset
    local_target = target - offset
    position = lax.iota(jnp.int32, count_pairs)
    earlier = (owner_ids[:, None] == owner_ids[None, :]) & (position[None, :] < position[:, None])
    slot_rank = jnp.sum(earlier.astype(jnp.int32), axis=1)
    slot_index = owner_ids * CAP + slot_rank
    left_tiles = jnp.take(tile_blocks, local_source, axis=2)
    right_tiles = jnp.take(tile_blocks, local_target, axis=2)
    cross = block_cross(left_tiles, right_tiles, divisor)
    slot_table = (
        jnp.zeros((band_size * CAP, TILE, 2 * bin_count), jnp.bfloat16).at[slot_index].set(cross)
    )
    arrived = lax.all_to_all(
        slot_table.reshape(band_size, CAP, TILE, 2 * bin_count),
        "band",
        split_axis=0,
        concat_axis=0,
        tiled=True,
    )

    def block_table(block_number):
        return lag_table(block_number * bin_count, bin_count, band_size * bin_count)

    all_weights = jax.vmap(block_table)(lax.iota(jnp.int32, band_size))
    added = jnp.einsum("bfg,boag->ofa", all_weights, arrived, preferred_element_type=jnp.float32)
    return stacks + added[None]


def solution(mesh):
    in_specs = (
        P(None, None, "chan", "band"),
        P(),
        P("chan", None, None),
        P("chan", None, None),
        P("chan", "band", None, None),
    )
    out_specs = P("chan", "band", None, None)
    return jax.shard_map(body, mesh=mesh, in_specs=in_specs, out_specs=out_specs, check_vma=False)
```

profile of v0, /device:TPU:1, one launch (start us, length us, event | category | flops | bytes accessed | tf_op | source)
XLA Modules:
  0.0 29.5 jit_solution(5717372996502331670)
XLA Ops:
  0.0 0.0 copy-start.3
  0.0 0.7 %copy-done.3 = s32[2,128]{1,0:T(2,128)S(1)} copy-done((s32[2,128]{1,0:T(2,128)S(1)}, s32[2,128]{1,0:T(2,128)}, u32[]{:S(2)}) %copy-start.3) | copy-done | bytes 1048
  0.7 0.1 dynamic-slice_convert_fusion
  0.8 0.1 broadcast_bitcast_fusion
  0.9 1.0 %convert_element_type.43 = f32[2,2,4096,8]{2,3,1,0:T(8,128)S(1)} convert(bf16[2,2,4096,8]{2,3,1,0:T(8,128)(2,1)} %param.7) | non-fusion elementwise | flops 131072 | bytes 786432 | tf_op jit(solution)/shard_map/convert_element_type | solution.py:43
  1.9 0.0 copy-start
  1.9 0.1 fusion.3
  2.0 0.0 copy-start.1
  2.0 0.8 %copy-done = bf16[2,2,4096,8]{2,3,1,0:T(8,128)(2,1)S(1)} copy-done((bf16[2,2,4096,8]{2,3,1,0:T(8,128)(2,1)S(1)}, bf16[2,2,4096,8]{2,3,1,0:T(8,128)(2,1)}, u32[]{:S(2)}) %copy-start) | copy-done | bytes 262168
  2.8 0.1 multiply_convert_fusion
  2.9 4.5 %collective-permute-start = (bf16[2,2,896,8]{2,3,1,0:T(8,128)(2,1)S(1)}, bf16[2,2,896,8]{2,3,1,0:T(8,128)(2,1)S(1)}, u32[]{:S(2)}, u32[]{:S(2)}) collective-permute-start(bf16[2,2,896,8]{2,3,1,0:T(8,128)(2,1)S(1)} %get-tuple-element.12), channel_id=1, source_target_pairs={{0,1},{1,2},{2,3},{4,5},{5,6},{6,7},{8,9},{9,10},{10,11},{12,13},{... | collective-permute-start | bytes 172040 | tf_op jit(solution)/shard_map/ppermute | solution.py:24
  7.4 1.9 %collective-permute-start.1 = (bf16[2,2,896,8]{2,3,1,0:T(8,128)(2,1)S(1)}, bf16[2,2,896,8]{2,3,1,0:T(8,128)(2,1)S(1)}, u32[]{:S(2)}, u32[]{:S(2)}) collective-permute-start(bf16[2,2,896,8]{2,3,1,0:T(8,128)(2,1)S(1)} %get-tuple-element.13), channel_id=1, source_target_pairs={{1,0},{2,1},{3,2},{5,4},{6,5},{7,6},{9,8},{10,9},{11,10},{13,12},{... | collective-permute-start | bytes 172040 | tf_op jit(solution)/shard_map/ppermute | solution.py:25
  9.4 0.0 copy-start.2
  9.4 0.7 %copy-done.2 = s32[1,8,2]{1,2,0:T(2,128)S(1)} copy-done((s32[1,8,2]{1,2,0:T(2,128)S(1)}, s32[1,8,2]{1,2,0:T(2,128)}, u32[]{:S(2)}) %copy-start.2) | copy-done | bytes 88
  10.1 0.2 fusion.15
  10.3 0.2 fusion.1
  10.5 0.0 copy-start.4
  10.5 0.6 %copy-done.4 = s32[1,8,1]{1,2,0:T(1,128)S(1)} copy-done((s32[1,8,1]{1,2,0:T(1,128)S(1)}, s32[1,8,1]{1,2,0:T(1,128)}, u32[]{:S(2)}) %copy-start.4) | copy-done | bytes 56
  11.1 0.2 convert_reduce_fusion
  11.3 0.1 iota_add_fusion
  11.4 0.0 copy-done.1
  11.4 0.2 copy.14
  11.6 0.0 collective-permute-done
  11.6 1.3 %collective-permute-done.1 = bf16[2,2,896,8]{2,3,1,0:T(8,128)(2,1)S(1)} collective-permute-done((bf16[2,2,896,8]{2,3,1,0:T(8,128)(2,1)S(1)}, bf16[2,2,896,8]{2,3,1,0:T(8,128)(2,1)S(1)}, u32[]{:S(2)}, u32[]{:S(2)}) %collective-permute-start.1) | collective-permute-done | bytes 57376 | tf_op jit(solution)/shard_map/ppermute | solution.py:25
  12.9 0.6 %gather_fusion = bf16[8,2,2,128,8]{3,4,2,1,0:T(8,128)(2,1)S(1)} fusion(bf16[2,2,46,128,8]{3,4,2,1,0:T(8,128)(2,1)S(1)} %maximum_bitcast_fusion, s32[1024]{0:T(1024)S(1)} %pad_clamp_fusion.1), kind=kCustom, calls=%fused_computation.clone | custom fusion | bytes 131104 | tf_op jit(solution)/shard_map/jit(_take)/gather | solution.py:92
  13.5 0.6 %gather_fusion.1 = bf16[8,2,2,128,8]{3,4,2,1,0:T(8,128)(2,1)S(1)} fusion(bf16[2,2,46,128,8]{3,4,2,1,0:T(8,128)(2,1)S(1)} %maximum_bitcast_fusion, s32[1024]{0:T(1024)S(1)} %pad_clamp_fusion), kind=kCustom, calls=%fused_computation.1.clone | custom fusion | bytes 131104 | tf_op jit(solution)/shard_map/jit(_take)/gather | solution.py:93
  14.1 0.1 select_bitcast_fusion
  14.2 0.1 fusion.13
  14.3 0.6 %broadcast_in_dim.15 = bf16[16,128,16]{1,2,0:T(8,128)(2,1)} broadcast(bf16[]{:T(256)} %constant.12.clone.1), dimensions={} | broadcast | bytes 65538 | tf_op jit(solution)/shard_map/broadcast_in_dim | solution.py:96
  14.9 2.0 %scatter_fusion = bf16[16,128,16]{1,2,0:T(8,128)(2,1)} fusion(bf16[16,128,16]{1,2,0:T(8,128)(2,1)} %broadcast_in_dim.15, s32[8]{0:T(128)S(1)} %fusion.20, bf16[8,128,16]{1,2,0:T(8,128)(2,1)S(1)} %fusion.13), kind=kCustom, calls=%fused_computation.2 | custom fusion | bytes 98336 | tf_op jit(solution)/shard_map/scatter | solution.py:96
  16.9 5.6 %all-to-all-start = ((bf16[8,2,128,16]{2,3,1,0:T(8,128)(2,1)}), bf16[8,2,128,16]{2,3,1,0:T(8,128)(2,1)S(1)}, u32[]{:S(2)}, u32[]{:S(2)}) async-start(bf16[8,2,128,16]{2,3,1,0:T(8,128)(2,1)} %bitcast.10), calls=%async_computation | async-start | bytes 131072 | tf_op jit(solution)/shard_map/all_to_all | solution.py:98
  22.5 0.6 %multiply_convert_fusion.2 = (bf16[8,512,8]{1,2,0:T(8,128)(2,1)S(1)}, bf16[8,512,8]{1,2,0:T(8,128)(2,1)S(1)}) fusion(s32[8,8]{1,0:T(8,128)S(1)} %iota_add_fusion, s32[512]{0:T(512)S(1)} %iota_add_fusion.1), kind=kLoop, calls=%fused_computation.25 | loop fusion | flops 622592 | bytes 133376 | tf_op jit(solution)/shard_map/convert
  23.1 5.2 %all-to-all-done = bf16[8,2,128,16]{2,3,1,0:T(8,128)(2,1)S(1)} async-done(((bf16[8,2,128,16]{2,3,1,0:T(8,128)(2,1)}), bf16[8,2,128,16]{2,3,1,0:T(8,128)(2,1)S(1)}, u32[]{:S(2)}, u32[]{:S(2)}) %all-to-all-start) | async-done | bytes 65568 | tf_op jit(solution)/shard_map/all_to_all | solution.py:98
  28.2 0.2 fusion
  28.5 1.0 %copy.15 = f32[1,2,512,128]{3,2,1,0:T(8,128)} copy(f32[1,2,512,128]{2,3,1,0:T(8,128)S(1)} %fusion) | data formatting | bytes 1048576 | tf_op jit(solution)/shard_map/add | solution.py:111
  (13 shorter events, 0.2 us)
Async XLA Ops:
  0.0 0.7 %copy-start.3 = (s32[2,128]{1,0:T(2,128)S(1)}, s32[2,128]{1,0:T(2,128)}, u32[]{:S(2)}) copy-start(s32[2,128]{1,0:T(2,128)} %param.8) | copy-start | bytes 3076
  1.9 1.0 %copy-start = (bf16[2,2,4096,8]{2,3,1,0:T(8,128)(2,1)S(1)}, bf16[2,2,4096,8]{2,3,1,0:T(8,128)(2,1)}, u32[]{:S(2)}) copy-start(bf16[2,2,4096,8]{2,3,1,0:T(8,128)(2,1)} %param.7) | copy-start | bytes 786436
  2.0 9.4 %copy-start.1 = (f32[1,2,512,128]{3,2,1,0:T(8,128)S(1)}, f32[1,2,512,128]{3,2,1,0:T(8,128)}, u32[]{:S(2)}) copy-start(f32[1,2,512,128]{3,2,1,0:T(8,128)} %param.11) | copy-start | bytes 1572868
  2.9 8.7 %collective-permute-start = (bf16[2,2,896,8]{2,3,1,0:T(8,128)(2,1)S(1)}, bf16[2,2,896,8]{2,3,1,0:T(8,128)(2,1)S(1)}, u32[]{:S(2)}, u32[]{:S(2)}) collective-permute-start(bf16[2,2,896,8]{2,3,1,0:T(8,128)(2,1)S(1)} %get-tuple-element.12), channel_id=1, source_target_pairs={{0,1},{1,2},{2,3},{4,5},{5,6},{6,7},{8,9},{9,10},{10,11},{12,13},{... | collective-permute-start | bytes 172040 | tf_op jit(solution)/shard_map/ppermute | solution.py:24
  7.4 5.5 %collective-permute-start.1 = (bf16[2,2,896,8]{2,3,1,0:T(8,128)(2,1)S(1)}, bf16[2,2,896,8]{2,3,1,0:T(8,128)(2,1)S(1)}, u32[]{:S(2)}, u32[]{:S(2)}) collective-permute-start(bf16[2,2,896,8]{2,3,1,0:T(8,128)(2,1)S(1)} %get-tuple-element.13), channel_id=1, source_target_pairs={{1,0},{2,1},{3,2},{5,4},{6,5},{7,6},{9,8},{10,9},{11,10},{13,12},{... | collective-permute-start | bytes 172040 | tf_op jit(solution)/shard_map/ppermute | solution.py:25
  9.4 0.7 %copy-start.2 = (s32[1,8,2]{1,2,0:T(2,128)S(1)}, s32[1,8,2]{1,2,0:T(2,128)}, u32[]{:S(2)}) copy-start(s32[1,8,2]{1,2,0:T(2,128)} %param.9) | copy-start | bytes 196
  10.5 0.7 %copy-start.4 = (s32[1,8,1]{1,2,0:T(1,128)S(1)}, s32[1,8,1]{1,2,0:T(1,128)}, u32[]{:S(2)}) copy-start(s32[1,8,1]{1,2,0:T(1,128)} %param.10) | copy-start | bytes 100
  16.9 11.3 %all-to-all-start = ((bf16[8,2,128,16]{2,3,1,0:T(8,128)(2,1)}), bf16[8,2,128,16]{2,3,1,0:T(8,128)(2,1)S(1)}, u32[]{:S(2)}, u32[]{:S(2)}) async-start(bf16[8,2,128,16]{2,3,1,0:T(8,128)(2,1)} %bitcast.10), calls=%async_computation | async-start | bytes 131072 | tf_op jit(solution)/shard_map/all_to_all | solution.py:98
where the time goes:
time: 29.8 us; the launch traced here: 29.5 us
  starting transfers between devices  12 us (40%)
  local copies, waits for them, and re-layouts  7.85 us (26%)
  waiting for transfers between devices  6.42 us (22%)
  other arithmetic  2.4 us (8%)
  matrix products  0.63 us (2%)
    all_to_all x1, starting transfers between devices, body(): lax.all_to_all(slot_table.reshape(band_size, CAP, TILE, 2 * bin_count), '...  5.55 us
    all_to_all x1, waiting for transfers between devices, body(): lax.all_to_all(slot_table.reshape(band_size, CAP, TILE, 2 * bin_count), '...  5.15 us
    ppermute x1, starting transfers between devices, padded(): before = lax.ppermute(last, axis, up)  4.5 us
    unnamed x13, local copies, waits for them, and re-layouts  3.09 us
    scatter x1, local copies, waits for them, and re-layouts, body(): jnp.zeros((band_size * CAP, TILE, 2 * bin_count), jnp.bfloat16)  1.96 us
    ppermute x1, starting transfers between devices, padded(): after = lax.ppermute(first, axis, down)  1.92 us
    ppermute x1, waiting for transfers between devices, padded(): after = lax.ppermute(first, axis, down)  1.27 us
    add x1, local copies, waits for them, and re-layouts, body(): return stacks + added[None]  1 us
  transfers between devices with their start and end apart: 3, of which 2 were waited for; matrix products, arithmetic and copies ran while one was open for 5% of the time, Pallas kernels for 0%

commit v1 on v0

v1 whole, which is shorter than its diff:
```python
import functools
import math

import jax
import jax.numpy as jnp
from jax import lax
from jax.experimental import pallas as pl
from jax.experimental.pallas import tpu as pltpu
from jax.sharding import PartitionSpec as P

TILE = 128
MAXOFF = 7
LAGS = 512
CAP = 2


STABILITY_FLOOR = 1e-05


def lag_weights(bin_count, band_size):
    total_bins = bin_count * band_size
    shape = (LAGS, 2 * total_bins)
    column = lax.broadcasted_iota(jnp.int32, shape, 1)
    lag_shift = lax.broadcasted_iota(jnp.int32, shape, 0) - LAGS // 2
    block, within = column // (2 * bin_count), column % (2 * bin_count)
    part, frequency = within // bin_count, block * bin_count + within % bin_count
    phase_index = jnp.mod(lag_shift * frequency, total_bins)
    angles = phase_index.astype(jnp.float32) * (2.0 * math.pi / total_bins)
    amplitude = 1.0 / math.sqrt(total_bins)
    return jnp.where(part == 0, jnp.cos(angles) * amplitude, -jnp.sin(angles) * amplitude).astype(
        jnp.bfloat16
    )


def halos(bins_first, quarter, quarters):
    length = bins_first.shape[3]
    width = MAXOFF * TILE
    first = lax.slice_in_dim(bins_first, 0, width, axis=3)
    last = lax.slice_in_dim(bins_first, length - width, length, axis=3)
    even = quarter % 2 == 0
    near_pairs = [(i, i ^ 1) for i in range(quarters)]
    far_pairs = [(i, (i + 1 if i % 2 else i - 1) % quarters) for i in range(quarters)]
    near = lax.ppermute(jnp.where(even, last, first), "chan", near_pairs)
    far = lax.ppermute(jnp.where(even, first, last), "chan", far_pairs)
    return near, far


def cross_kernel(pairs, owners, flags, own, near, far, out, held):
    windows, bins = own.shape[0], own.shape[2]
    tiles_here = own.shape[3] // TILE
    quarter = lax.axis_index("chan")
    even = lax.rem(quarter, 2) == 0
    base = quarter * tiles_here

    def clear(o, carry):
        held[o] = 0
        return carry

    lax.fori_loop(0, held.shape[0], clear, 0)
    out[...] = jnp.zeros_like(out)

    def tile_of(ref, index):
        start = pl.multiple_of(index * TILE, TILE)
        return ref[:, :, :, pl.ds(start, TILE)].astype(jnp.float32)

    def whiten(values, tile):
        energy = values[:, 0] * values[:, 0] + values[:, 1] * values[:, 1]
        level = jnp.sqrt(jnp.mean(energy, axis=1, keepdims=True) + STABILITY_FLOOR)
        rows = []
        for w in range(windows):
            gate = flags[w, tile].astype(jnp.float32)
            rows.append((values[w] / level[w][None] * gate).astype(jnp.bfloat16).astype(jnp.float32))
        return rows

    def one_pair(p, carry):
        source, target, owner = pairs[0, p], pairs[1, p], owners[0, p]
        here = target - base
        below, above = here < 0, here >= tiles_here
        end = MAXOFF - 1
        below_at = jnp.clip(here + MAXOFF, 0, end)
        above_at = jnp.clip(here - tiles_here, 0, end)
        beside_near = jnp.where(even, above, below)
        beside_far = jnp.where(even, below, above)
        right = tile_of(own, jnp.clip(here, 0, tiles_here - 1))
        right = jnp.where(beside_near, tile_of(near, jnp.where(even, above_at, below_at)), right)
        right = jnp.where(beside_far, tile_of(far, jnp.where(even, below_at, above_at)), right)
        left = whiten(tile_of(own, source - base), source)
        right = whiten(right, target)
        real = imag = None
        together = 0
        for w in range(windows):
            together = together + flags[w, source] * flags[w, target]
            re = left[w][0] * right[w][0] + left[w][1] * right[w][1]
            im = left[w][0] * right[w][1] - left[w][1] * right[w][0]
            real = re if real is None else real + re
            imag = im if imag is None else imag + im
        divisor = jnp.maximum(together, 1).astype(jnp.float32)
        rank = held[owner]
        held[owner] = rank + 1
        spectrum = jnp.concatenate([real, imag], axis=0) / divisor
        out[owner * CAP + rank] = spectrum.astype(jnp.bfloat16)
        return carry

    count = pairs.shape[1]
    lax.fori_loop(0, count, one_pair, 0, unroll=count <= 8)


def in_vmem(array):
    return pltpu.with_memory_space_constraint(array, pltpu.VMEM)


def cross_table(bins_first, near, far, window_flags, pair_list, owner_ids, band_size):
    bins = bins_first.shape[2]
    smem = pl.BlockSpec(memory_space=pltpu.SMEM)
    vmem = pl.BlockSpec(memory_space=pltpu.VMEM)
    return pl.pallas_call(
        cross_kernel,
        out_shape=pltpu.VMEM((band_size * CAP, 2 * bins, TILE), jnp.bfloat16),
        in_specs=[smem, smem, smem, vmem, vmem, vmem],
        out_specs=vmem,
        scratch_shapes=[pltpu.SMEM((band_size,), jnp.int32)],
        name="cross",
    )(pair_list, owner_ids, window_flags, bins_first, in_vmem(near), in_vmem(far))


def stack_kernel(weights, arrived, stacks, out):
    columns = arrived.shape[0] * arrived.shape[2]
    for s in range(arrived.shape[1]):
        spectrum = arrived[:, s].reshape(columns, TILE)
        added = jnp.dot(weights[...], spectrum, preferred_element_type=jnp.float32)
        out[s] = stacks[s] + added


def stack_lags(weights, arrived, stacks):
    vmem = pl.BlockSpec(memory_space=pltpu.VMEM)
    return pl.pallas_call(
        stack_kernel,
        out_shape=jax.ShapeDtypeStruct(stacks.shape, stacks.dtype),
        in_specs=[vmem, vmem, vmem],
        out_specs=vmem,
        name="stack",
    )(in_vmem(weights), in_vmem(arrived), stacks)


def body(spectra, window_flags, pair_tiles, owners, stacks):
    quarter = lax.axis_index("chan")
    band_size, quarters = lax.axis_size("band"), lax.axis_size("chan")
    bins = spectra.shape[3]
    bins_first = jnp.transpose(spectra, (0, 1, 3, 2))
    near, far = halos(bins_first, quarter, quarters)
    table = cross_table(bins_first, near, far, window_flags, pair_tiles[0].T, owners[0].T, band_size)
    arrived = lax.all_to_all(
        table.reshape(band_size, CAP, 2 * bins, TILE), "band", split_axis=0, concat_axis=0, tiled=True
    )
    weights = lag_weights(bins, band_size)
    return stack_lags(weights, arrived, stacks[0])[None]


def solution(mesh):
    in_specs = (
        P(None, None, "chan", "band"),
        P(),
        P("chan", None, None),
        P("chan", None, None),
        P("chan", "band", None, None),
    )
    out_specs = P("chan", "band", None, None)
    return jax.shard_map(body, mesh=mesh, in_specs=in_specs, out_specs=out_specs, check_vma=False)
```

time: 29.8 us -> 23.5 us (0.79)
  the two profiles are of different devices: /device:TPU:1 before, /device:TPU:0 now
where the time goes in v1:
time: 23.5 us; the launch traced here: 23.2 us
  starting transfers between devices  9.91 us (42%)
  waiting for transfers between devices  7.25 us (31%)
  Pallas kernels  3.91 us (17%)
  other arithmetic  2.14 us (9%)
    all_to_all x1, starting transfers between devices, body(): lax.all_to_all(table.reshape(band_size, CAP, 2 * bins, TILE), 'band', spl...  6.76 us
    all_to_all x1, waiting for transfers between devices, body(): lax.all_to_all(table.reshape(band_size, CAP, 2 * bins, TILE), 'band', spl...  5.64 us
    ppermute x1, starting transfers between devices, halos(): far = lax.ppermute(jnp.where(even, first, last), 'chan', far_pairs)  2.47 us
    pallas_call x1, Pallas kernels, stack_lags(): pl.pallas_call(stack_kernel, out_shape=jax.ShapeDtypeStruct(stacks.shape,...  2.04 us
    pallas_call x1, Pallas kernels, cross_table(): pl.pallas_call(cross_kernel, out_shape=pltpu.VMEM((band_size * CAP, 2 * b...  1.87 us
    ppermute x1, waiting for transfers between devices, halos(): far = lax.ppermute(jnp.where(even, first, last), 'chan', far_pairs)  1.61 us
    convert_element_type x1, other arithmetic, lag_weights(): jnp.where(part == 0, jnp.cos(angles) * amplitude, -jnp.sin(angles) * ampl...  1.26 us
    select_n x1, other arithmetic, halos(): far = lax.ppermute(jnp.where(even, first, last), 'chan', far_pairs)  0.86 us
  transfers between devices with their start and end apart: 3, of which 2 were waited for; matrix products, arithmetic and copies ran while one was open for 6% of the time, Pallas kernels for 0%

profile of v1, /device:TPU:0, one launch (start us, length us, event | category | flops | bytes accessed | tf_op | source)
XLA Modules:
  0.0 23.2 jit_solution(4426422692983895228)
XLA Ops:
  0.0 0.9 %broadcast_select_fusion = (bf16[2,2,8,896]{3,2,1,0:T(8,128)(2,1)S(1)}, bf16[2,2,8,896]{3,2,1,0:T(8,128)(2,1)S(1)}) fusion(pred[]{:T(512)S(6)} %eq.14, bf16[2,2,8,4096]{3,2,1,0:T(8,128)(2,1)} %bitcast.8), kind=kLoop, calls=%fused_computation.22 | loop fusion | flops 57344 | bytes 229377 | tf_op jit(solution)/shard_map/jit(_where)/select_n | solution.py:44
  0.9 2.5 %collective-permute-start.1 = (bf16[2,2,8,896]{3,2,1,0:T(8,128)(2,1)S(1)}, bf16[2,2,8,896]{3,2,1,0:T(8,128)(2,1)S(1)}, u32[]{:S(2)}, u32[]{:S(2)}) collective-permute-start(bf16[2,2,8,896]{3,2,1,0:T(8,128)(2,1)S(1)} %get-tuple-element.5), channel_id=1, source_target_pairs={{0,3},{1,2},{2,1},{3,0},{4,7},{5,6},{6,5},{7,4},{8,11},{9,10},{10,... | collective-permute-start | bytes 172040 | tf_op jit(solution)/shard_map/ppermute | solution.py:44
  3.3 0.7 %collective-permute-start = (bf16[2,2,8,896]{3,2,1,0:T(8,128)(2,1)S(1)}, bf16[2,2,8,896]{3,2,1,0:T(8,128)(2,1)S(1)}, u32[]{:S(2)}, u32[]{:S(2)}) collective-permute-start(bf16[2,2,8,896]{3,2,1,0:T(8,128)(2,1)S(1)} %get-tuple-element.6), channel_id=1, source_target_pairs={{0,1},{1,0},{2,3},{3,2},{4,5},{5,4},{6,7},{7,6},{8,9},{9,8},{10,11... | collective-permute-start | bytes 172040 | tf_op jit(solution)/shard_map/ppermute | solution.py:43
  4.0 1.6 %collective-permute-done.1.far = bf16[2,2,8,896]{3,2,1,0:T(8,128)(2,1)S(1)} collective-permute-done((bf16[2,2,8,896]{3,2,1,0:T(8,128)(2,1)S(1)}, bf16[2,2,8,896]{3,2,1,0:T(8,128)(2,1)S(1)}, u32[]{:S(2)}, u32[]{:S(2)}) %collective-permute-start.1) | collective-permute-done | bytes 57376 | tf_op jit(solution)/shard_map/ppermute | solution.py:44
  5.6 0.0 collective-permute-done.near
  5.7 1.9 %cross.1 = bf16[16,16,128]{2,1,0:T(8,128)(2,1)} custom-call(s32[2,8]{1,0:T(2,128)} %bitcast.11, s32[1,8]{1,0:T(1,128)} %bitcast.12, s32[2,128]{1,0:T(2,128)} %flags.1, bf16[2,2,8,4096]{3,2,1,0:T(8,128)(2,1)} %bitcast.9, bf16[2,2,8,896]{3,2,1,0:T(8,128)(2,1)S(1)} %collective-permute-done.near, bf16[2,2,8,896]{3,2,1,0:T(8,128)(2,1)S(1)} %collective-permute-done.1.far), custom_call_target="tpu_custom_call" | custom-call | tf_op jit(solution)/shard_map/cross/pallas_call | solution.py:116
  7.5 6.8 %all-to-all-start = ((bf16[8,2,16,128]{3,2,1,0:T(8,128)(2,1)}), bf16[8,2,16,128]{3,2,1,0:T(8,128)(2,1)S(1)}, u32[]{:S(2)}, u32[]{:S(2)}) async-start(bf16[8,2,16,128]{3,2,1,0:T(8,128)(2,1)} %bitcast.4), calls=%async_computation | async-start | bytes 131072 | tf_op jit(solution)/shard_map/all_to_all | solution.py:152
  14.3 1.3 %select_convert_fusion.weights = bf16[512,128]{1,0:T(8,128)(2,1)S(1)} fusion(s32[128]{0:T(128)S(1)} %get-tuple-element.9, s32[128]{0:T(128)S(1)} %get-tuple-element.11, s32[512]{0:T(512)S(1)} %iota_add_fusion, s32[128]{0:T(128)S(1)} %get-tuple-element.10, s32[128]{0:T(128)S(1)} %get-tuple-element.12, pred[128]{0:T(512)(128)(4,1)S(1)} %get-tuple-element.7, ...), kind=kLoop, calls=%fused_computation.20 | loop fusion | flops 2818048 | bytes 135424 | tf_op jit(solution)/shard_map/convert_element_type | solution.py:30
  15.6 5.6 %all-to-all-done.arrived = bf16[8,2,16,128]{3,2,1,0:T(8,128)(2,1)S(1)} async-done(((bf16[8,2,16,128]{3,2,1,0:T(8,128)(2,1)}), bf16[8,2,16,128]{3,2,1,0:T(8,128)(2,1)S(1)}, u32[]{:S(2)}, u32[]{:S(2)}) %all-to-all-start) | async-done | bytes 65568 | tf_op jit(solution)/shard_map/all_to_all | solution.py:152
  21.2 2.0 %stack.1 = f32[2,512,128]{2,1,0:T(8,128)} custom-call(bf16[512,128]{1,0:T(8,128)(2,1)S(1)} %select_convert_fusion.weights, bf16[8,2,16,128]{3,2,1,0:T(8,128)(2,1)S(1)} %all-to-all-done.arrived, f32[2,512,128]{2,1,0:T(8,128)} %bitcast.10), custom_call_target="tpu_custom_call" | custom-call | tf_op jit(solution)/shard_map/stack/pallas_call | solution.py:136
  (4 shorter events, 0.0 us)
Async XLA Ops:
  0.9 4.8 %collective-permute-start.1 = (bf16[2,2,8,896]{3,2,1,0:T(8,128)(2,1)S(1)}, bf16[2,2,8,896]{3,2,1,0:T(8,128)(2,1)S(1)}, u32[]{:S(2)}, u32[]{:S(2)}) collective-permute-start(bf16[2,2,8,896]{3,2,1,0:T(8,128)(2,1)S(1)} %get-tuple-element.5), channel_id=1, source_target_pairs={{0,3},{1,2},{2,1},{3,0},{4,7},{5,6},{6,5},{7,4},{8,11},{9,10},{10,... | collective-permute-start | bytes 172040 | tf_op jit(solution)/shard_map/ppermute | solution.py:44
  3.3 2.3 %collective-permute-start = (bf16[2,2,8,896]{3,2,1,0:T(8,128)(2,1)S(1)}, bf16[2,2,8,896]{3,2,1,0:T(8,128)(2,1)S(1)}, u32[]{:S(2)}, u32[]{:S(2)}) collective-permute-start(bf16[2,2,8,896]{3,2,1,0:T(8,128)(2,1)S(1)} %get-tuple-element.6), channel_id=1, source_target_pairs={{0,1},{1,0},{2,3},{3,2},{4,5},{5,4},{6,7},{7,6},{8,9},{9,8},{10,11... | collective-permute-start | bytes 172040 | tf_op jit(solution)/shard_map/ppermute | solution.py:43
  7.5 13.7 %all-to-all-start = ((bf16[8,2,16,128]{3,2,1,0:T(8,128)(2,1)}), bf16[8,2,16,128]{3,2,1,0:T(8,128)(2,1)S(1)}, u32[]{:S(2)}, u32[]{:S(2)}) async-start(bf16[8,2,16,128]{3,2,1,0:T(8,128)(2,1)} %bitcast.4), calls=%async_computation | async-start | bytes 131072 | tf_op jit(solution)/shard_map/all_to_all | solution.py:152

commit v2 on v1

--- a/solution.py
+++ b/solution.py
@@ -12,18 +12,19 @@
 MAXOFF = 7
 LAGS = 512
 CAP = 2
+KERNEL_VMEM = 16 * 2**20
 
 
 STABILITY_FLOOR = 1e-05
 
 
-def lag_weights(bin_count, band_size):
+def lag_weights(bin_count, band_size, band):
     total_bins = bin_count * band_size
     shape = (LAGS, 2 * total_bins)
     column = lax.broadcasted_iota(jnp.int32, shape, 1)
     lag_shift = lax.broadcasted_iota(jnp.int32, shape, 0) - LAGS // 2
     block, within = column // (2 * bin_count), column % (2 * bin_count)
-    part, frequency = within // bin_count, block * bin_count + within % bin_count
+    part, frequency = within // bin_count, (block ^ band) * bin_count + within % bin_count
     phase_index = jnp.mod(lag_shift * frequency, total_bins)
     angles = phase_index.astype(jnp.float32) * (2.0 * math.pi / total_bins)
     amplitude = 1.0 / math.sqrt(total_bins)
@@ -48,7 +49,7 @@
 def cross_kernel(pairs, owners, flags, own, near, far, out, held):
     windows, bins = own.shape[0], own.shape[2]
     tiles_here = own.shape[3] // TILE
-    quarter = lax.axis_index("chan")
+    quarter, band = lax.axis_index("chan"), lax.axis_index("band")
     even = lax.rem(quarter, 2) == 0
     base = quarter * tiles_here
 
@@ -98,7 +99,7 @@
         rank = held[owner]
         held[owner] = rank + 1
         spectrum = jnp.concatenate([real, imag], axis=0) / divisor
-        out[owner * CAP + rank] = spectrum.astype(jnp.bfloat16)
+        out[(owner ^ band) * CAP + rank] = spectrum.astype(jnp.bfloat16)
         return carry
 
     count = pairs.shape[1]
@@ -107,6 +108,10 @@
 
 def in_vmem(array):
     return pltpu.with_memory_space_constraint(array, pltpu.VMEM)
+
+
+def in_smem(array):
+    return pltpu.with_memory_space_constraint(array, pltpu.SMEM)
 
 
 def cross_table(bins_first, near, far, window_flags, pair_list, owner_ids, band_size):
@@ -119,16 +124,38 @@
         in_specs=[smem, smem, smem, vmem, vmem, vmem],
         out_specs=vmem,
         scratch_shapes=[pltpu.SMEM((band_size,), jnp.int32)],
+        compiler_params=pltpu.CompilerParams(vmem_limit_bytes=KERNEL_VMEM),
         name="cross",
-    )(pair_list, owner_ids, window_flags, bins_first, in_vmem(near), in_vmem(far))
+    )(in_smem(pair_list), in_smem(owner_ids), in_smem(window_flags), in_vmem(bins_first), in_vmem(near), in_vmem(far))
 
 
-def stack_kernel(weights, arrived, stacks, out):
+def exchange(table, band_size):
+    held = table[None]
+    for stage in range(band_size.bit_length() - 1):
+        pairs = [(i, i ^ (1 << stage)) for i in range(band_size)]
+        split = held.reshape(held.shape[0], held.shape[1] // 2, 2, *held.shape[2:])
+        came = lax.ppermute(split[:, :, 1], "band", pairs)
+        held = jnp.concatenate([split[:, :, 0], came], axis=0)
+    return held[:, 0]
+
+
+def stack_kernel(weights, arrived, stacks, out, sums, sems):
     columns = arrived.shape[0] * arrived.shape[2]
+    lags = sums.shape[1]
+    parts = sems.shape[1]
+    rows = lags // parts
+    copies = []
     for s in range(arrived.shape[1]):
         spectrum = arrived[:, s].reshape(columns, TILE)
-        added = jnp.dot(weights[...], spectrum, preferred_element_type=jnp.float32)
-        out[s] = stacks[s] + added
+        for part in range(parts):
+            here = pl.ds(part * rows, rows)
+            added = jnp.dot(weights[here, :], spectrum, preferred_element_type=jnp.float32)
+            sums[s, here, :] = stacks[s, here, :] + added
+            copy = pltpu.make_async_copy(sums.at[s, here, :], out.at[s, here, :], sems.at[s, part])
+            copy.start()
+            copies.append(copy)
+    for copy in copies:
+        copy.wait()
 
 
 def stack_lags(weights, arrived, stacks):
@@ -137,9 +164,14 @@
         stack_kernel,
         out_shape=jax.ShapeDtypeStruct(stacks.shape, stacks.dtype),
         in_specs=[vmem, vmem, vmem],
-        out_specs=vmem,
+        out_specs=pl.BlockSpec(memory_space=pl.ANY),
+        scratch_shapes=[
+            pltpu.VMEM(stacks.shape, stacks.dtype),
+            pltpu.SemaphoreType.DMA((stacks.shape[0], 2)),
+        ],
+        compiler_params=pltpu.CompilerParams(vmem_limit_bytes=KERNEL_VMEM),
         name="stack",
-    )(in_vmem(weights), in_vmem(arrived), stacks)
+    )(in_vmem(weights), in_vmem(arrived), in_vmem(stacks))
 
 
 def body(spectra, window_flags, pair_tiles, owners, stacks):
@@ -149,10 +181,8 @@
     bins_first = jnp.transpose(spectra, (0, 1, 3, 2))
     near, far = halos(bins_first, quarter, quarters)
     table = cross_table(bins_first, near, far, window_flags, pair_tiles[0].T, owners[0].T, band_size)
-    arrived = lax.all_to_all(
-        table.reshape(band_size, CAP, 2 * bins, TILE), "band", split_axis=0, concat_axis=0, tiled=True
-    )
-    weights = lag_weights(bins, band_size)
+    arrived = exchange(table.reshape(band_size, CAP, 2 * bins, TILE), band_size)
+    weights = lag_weights(bins, band_size, lax.axis_index("band"))
     return stack_lags(weights, arrived, stacks[0])[None]
 
 

time: 23.5 us -> 21.9 us (0.932)
  Pallas kernels: 3.91 us -> 1.85 us
  waiting for transfers between devices: 7.25 us -> 6.03 us
  starting transfers between devices: 9.91 us -> 10.9 us
  local copies, waits for them, and re-layouts: 0 us -> 0.7 us
    ppermute x0 -> x3, starting transfers between devices: none -> 7.76 us  [exchange(): came = lax.ppermute(split[:, :, 1], 'band', pairs)]
    all_to_all x1 -> x0, starting transfers between devices: 6.76 us -> none  [body(): lax.all_to_all(table.reshape(band_size, CAP, 2 * bins, TILE), 'band', spl...]
    all_to_all x1 -> x0, waiting for transfers between devices: 5.64 us -> none  [body(): lax.all_to_all(table.reshape(band_size, CAP, 2 * bins, TILE), 'band', spl...]
    ppermute x0 -> x3, waiting for transfers between devices: none -> 4.4 us  [exchange(): came = lax.ppermute(split[:, :, 1], 'band', pairs)]
    pallas_call x1, Pallas kernels: 2.04 us -> 1 us  [stack_lags(): pl.pallas_call(stack_kernel, out_shape=jax.ShapeDtypeStruct(stacks.shape,...]
    pallas_call x1, Pallas kernels: 1.87 us -> 0.86 us  [cross_table(): pl.pallas_call(cross_kernel, out_shape=pltpu.VMEM((band_size * CAP, 2 * b...]
    unnamed x0 -> x12, local copies, waits for them, and re-layouts: none -> 0.69 us
  transfers between devices with their start and end apart: 3 -> 5, of which waited for: 2 -> 4; matrix products, arithmetic and copies ran while one was open for 6% -> 6% of each run, Pallas kernels for 0% -> 0%
where the time goes in v2:
time: 21.9 us; the launch traced here: 21.8 us
  starting transfers between devices  10.9 us (50%)
  waiting for transfers between devices  6.03 us (28%)
  other arithmetic  2.2 us (10%)
  Pallas kernels  1.85 us (8%)
  local copies, waits for them, and re-layouts  0.7 us (3%)
    ppermute x3, starting transfers between devices, exchange(): came = lax.ppermute(split[:, :, 1], 'band', pairs)  7.76 us
    ppermute x3, waiting for transfers between devices, exchange(): came = lax.ppermute(split[:, :, 1], 'band', pairs)  4.4 us
    ppermute x1, starting transfers between devices, halos(): far = lax.ppermute(jnp.where(even, first, last), 'chan', far_pairs)  2.47 us
    ppermute x1, waiting for transfers between devices, halos(): far = lax.ppermute(jnp.where(even, first, last), 'chan', far_pairs)  1.62 us
    convert_element_type x1, other arithmetic, lag_weights(): jnp.where(part == 0, jnp.cos(angles) * amplitude, -jnp.sin(angles) * ampl...  1.25 us
    pallas_call x1, Pallas kernels, stack_lags(): pl.pallas_call(stack_kernel, out_shape=jax.ShapeDtypeStruct(stacks.shape,...  1 us
    select_n x1, other arithmetic, halos(): far = lax.ppermute(jnp.where(even, first, last), 'chan', far_pairs)  0.91 us
    pallas_call x1, Pallas kernels, cross_table(): pl.pallas_call(cross_kernel, out_shape=pltpu.VMEM((band_size * CAP, 2 * b...  0.86 us
  transfers between devices with their start and end apart: 5, of which 4 were waited for; matrix products, arithmetic and copies ran while one was open for 6% of the time, Pallas kernels for 0%

profile of v2, /device:TPU:0, one launch (start us, length us, event | category | flops | bytes accessed | tf_op | source)
XLA Modules:
  0.0 21.8 jit_solution(12716421662243035406)
XLA Ops:
  0.0 0.0 copy-start
  0.0 0.9 %broadcast_select_fusion = (bf16[2,2,8,896]{3,2,1,0:T(8,128)(2,1)S(1)}, bf16[2,2,8,896]{3,2,1,0:T(8,128)(2,1)S(1)}) fusion(pred[]{:T(512)S(6)} %eq.14, bf16[2,2,8,4096]{3,2,1,0:T(8,128)(2,1)} %bitcast.30), kind=kLoop, calls=%fused_computation.26 | loop fusion | flops 57344 | bytes 229377 | tf_op jit(solution)/shard_map/jit(_where)/select_n | solution.py:45
  0.9 2.5 %collective-permute-start.1 = (bf16[2,2,8,896]{3,2,1,0:T(8,128)(2,1)S(1)}, bf16[2,2,8,896]{3,2,1,0:T(8,128)(2,1)S(1)}, u32[]{:S(2)}, u32[]{:S(2)}) collective-permute-start(bf16[2,2,8,896]{3,2,1,0:T(8,128)(2,1)S(1)} %get-tuple-element.5), channel_id=1, source_target_pairs={{0,3},{1,2},{2,1},{3,0},{4,7},{5,6},{6,5},{7,4},{8,11},{9,10},{10,... | collective-permute-start | bytes 172040 | tf_op jit(solution)/shard_map/ppermute | solution.py:45
  3.4 0.7 %collective-permute-start = (bf16[2,2,8,896]{3,2,1,0:T(8,128)(2,1)S(1)}, bf16[2,2,8,896]{3,2,1,0:T(8,128)(2,1)S(1)}, u32[]{:S(2)}, u32[]{:S(2)}) collective-permute-start(bf16[2,2,8,896]{3,2,1,0:T(8,128)(2,1)S(1)} %get-tuple-element.6), channel_id=1, source_target_pairs={{0,1},{1,0},{2,3},{3,2},{4,5},{5,4},{6,7},{7,6},{8,9},{9,8},{10,11... | collective-permute-start | bytes 172040 | tf_op jit(solution)/shard_map/ppermute | solution.py:44
  4.1 0.0 copy-start.3
  4.1 1.6 %collective-permute-done.1.far = bf16[2,2,8,896]{3,2,1,0:T(8,128)(2,1)S(1)} collective-permute-done((bf16[2,2,8,896]{3,2,1,0:T(8,128)(2,1)S(1)}, bf16[2,2,8,896]{3,2,1,0:T(8,128)(2,1)S(1)}, u32[]{:S(2)}, u32[]{:S(2)}) %collective-permute-start.1) | collective-permute-done | bytes 57376 | tf_op jit(solution)/shard_map/ppermute | solution.py:45
  5.7 0.0 collective-permute-done.near
  5.7 0.0 copy-start.2
  5.7 0.0 copy-start.4
  5.7 0.0 copy-done
  5.7 0.0 copy-done.3
  5.7 0.7 %copy-done.2 = s32[1,8,2]{1,2,0:T(2,128)S(1)} copy-done((s32[1,8,2]{1,2,0:T(2,128)S(1)}, s32[1,8,2]{1,2,0:T(2,128)}, u32[]{:S(2)}) %copy-start.2) | copy-done | bytes 88
  6.4 0.0 copy-done.4
  6.4 0.9 %cross.1 = bf16[16,16,128]{2,1,0:T(8,128)(2,1)S(1)} custom-call(s32[2,8]{1,0:T(2,128)S(1)} %bitcast.34, s32[1,8]{1,0:T(1,128)S(1)} %bitcast.35, s32[2,128]{1,0:T(2,128)S(1)} %copy-done.3, bf16[2,2,8,4096]{3,2,1,0:T(8,128)(2,1)S(1)} %bitcast.31, bf16[2,2,8,896]{3,2,1,0:T(8,128)(2,1)S(1)} %collective-permute-done.near, ...), custom_call_target="tpu_custom_call" | custom-call | tf_op jit(solution)/shard_map/cross/pallas_call | solution.py:121
  7.2 0.0 copy-start.1
  7.3 2.5 %collective-permute-start.2 = (bf16[1,4,2,16,128]{4,3,2,1,0:T(8,128)(2,1)S(1)}, bf16[1,4,2,16,128]{4,3,2,1,0:T(8,128)(2,1)S(1)}, u32[]{:S(2)}, u32[]{:S(2)}) collective-permute-start(bf16[1,4,2,16,128]{4,3,2,1,0:T(8,128)(2,1)S(1)} %get-tuple-element.12), channel_id=1, source_target_pairs={{0,4},{4,0},{8,12},{12,8},{16,20},{20,16},{24,28},{28,24},{1,5},{5... | collective-permute-start | bytes 98312 | tf_op jit(solution)/shard_map/ppermute | solution.py:137
  9.8 1.9 %collective-permute-done.2 = bf16[1,4,2,16,128]{4,3,2,1,0:T(8,128)(2,1)S(1)} collective-permute-done((bf16[1,4,2,16,128]{4,3,2,1,0:T(8,128)(2,1)S(1)}, bf16[1,4,2,16,128]{4,3,2,1,0:T(8,128)(2,1)S(1)}, u32[]{:S(2)}, u32[]{:S(2)}) %collective-permute-start.2) | collective-permute-done | bytes 32800 | tf_op jit(solution)/shard_map/ppermute | solution.py:137
  11.7 2.1 %collective-permute-start.3 = (bf16[2,2,2,16,128]{4,3,2,0,1:T(8,128)(2,1)S(1)}, bf16[2,2,2,16,128]{4,3,2,0,1:T(8,128)(2,1)S(1)}, u32[]{:S(2)}, u32[]{:S(2)}) collective-permute-start(bf16[2,2,2,16,128]{4,3,2,0,1:T(8,128)(2,1)S(1)} %bitcast.38), channel_id=1, source_target_pairs={{0,8},{4,12},{8,0},{12,4},{16,24},{20,28},{24,16},{28,20},{1,9},{5... | collective-permute-start | bytes 98312 | tf_op jit(solution)/shard_map/ppermute | solution.py:137
  13.9 1.9 %collective-permute-done.3 = bf16[2,2,2,16,128]{4,3,2,0,1:T(8,128)(2,1)S(1)} collective-permute-done((bf16[2,2,2,16,128]{4,3,2,0,1:T(8,128)(2,1)S(1)}, bf16[2,2,2,16,128]{4,3,2,0,1:T(8,128)(2,1)S(1)}, u32[]{:S(2)}, u32[]{:S(2)}) %collective-permute-start.3) | collective-permute-done | bytes 32800 | tf_op jit(solution)/shard_map/ppermute | solution.py:137
  15.8 3.1 %collective-permute-start.4 = (bf16[4,1,2,16,128]{4,3,2,0,1:T(8,128)(2,1)S(1)}, bf16[4,1,2,16,128]{4,3,2,0,1:T(8,128)(2,1)S(1)}, u32[]{:S(2)}, u32[]{:S(2)}) collective-permute-start(bf16[4,1,2,16,128]{4,3,2,0,1:T(8,128)(2,1)S(1)} %get-tuple-element.8), channel_id=1, source_target_pairs={{0,16},{4,20},{8,24},{12,28},{16,0},{20,4},{24,8},{28,12},{1,17},{... | collective-permute-start | bytes 98312 | tf_op jit(solution)/shard_map/ppermute | solution.py:137
  18.9 1.3 %select_convert_fusion.weights = bf16[512,128]{1,0:T(8,128)(2,1)S(1)} fusion(s32[]{:T(128)S(6)} %axis_index.23, s32[128]{0:T(128)S(1)} %get-tuple-element.15, s32[128]{0:T(128)S(1)} %get-tuple-element.17, s32[512]{0:T(512)S(1)} %iota_add_fusion, s32[128]{0:T(128)S(1)} %get-tuple-element.16, s32[128]{0:T(128)S(1)} %get-tuple-element.18, ...), kind=kLoop, calls=%fused_computation.20 | loop fusion | flops 2883584 | bytes 135428 | tf_op jit(solution)/shard_map/convert_element_type | solution.py:31
  20.1 0.6 %collective-permute-done.4 = bf16[4,1,2,16,128]{4,3,2,0,1:T(8,128)(2,1)S(1)} collective-permute-done((bf16[4,1,2,16,128]{4,3,2,0,1:T(8,128)(2,1)S(1)}, bf16[4,1,2,16,128]{4,3,2,0,1:T(8,128)(2,1)S(1)}, u32[]{:S(2)}, u32[]{:S(2)}) %collective-permute-start.4) | collective-permute-done | bytes 32800 | tf_op jit(solution)/shard_map/ppermute | solution.py:137
  20.8 0.0 copy-done.1
  20.8 1.0 %stack.1 = f32[2,512,128]{2,1,0:T(8,128)} custom-call(bf16[512,128]{1,0:T(8,128)(2,1)S(1)} %select_convert_fusion.weights, bf16[8,2,16,128]{3,2,1,0:T(8,128)(2,1)S(1)} %maximum_bitcast_fusion.1.arrived, f32[2,512,128]{2,1,0:T(8,128)S(1)} %bitcast.32), custom_call_target="tpu_custom_call" | custom-call | tf_op jit(solution)/shard_map/stack/pallas_call | solution.py:163
  (11 shorter events, 0.1 us)
Async XLA Ops:
  0.0 5.7 %copy-start = (bf16[2,2,4096,8]{2,3,1,0:T(8,128)(2,1)S(1)}, bf16[2,2,4096,8]{2,3,1,0:T(8,128)(2,1)}, u32[]{:S(2)}) copy-start(bf16[2,2,4096,8]{2,3,1,0:T(8,128)(2,1)} %param.5) | copy-start | bytes 786436
  0.9 4.8 %collective-permute-start.1 = (bf16[2,2,8,896]{3,2,1,0:T(8,128)(2,1)S(1)}, bf16[2,2,8,896]{3,2,1,0:T(8,128)(2,1)S(1)}, u32[]{:S(2)}, u32[]{:S(2)}) collective-permute-start(bf16[2,2,8,896]{3,2,1,0:T(8,128)(2,1)S(1)} %get-tuple-element.5), channel_id=1, source_target_pairs={{0,3},{1,2},{2,1},{3,0},{4,7},{5,6},{6,5},{7,4},{8,11},{9,10},{10,... | collective-permute-start | bytes 172040 | tf_op jit(solution)/shard_map/ppermute | solution.py:45
  3.4 2.3 %collective-permute-start = (bf16[2,2,8,896]{3,2,1,0:T(8,128)(2,1)S(1)}, bf16[2,2,8,896]{3,2,1,0:T(8,128)(2,1)S(1)}, u32[]{:S(2)}, u32[]{:S(2)}) collective-permute-start(bf16[2,2,8,896]{3,2,1,0:T(8,128)(2,1)S(1)} %get-tuple-element.6), channel_id=1, source_target_pairs={{0,1},{1,0},{2,3},{3,2},{4,5},{5,4},{6,7},{7,6},{8,9},{9,8},{10,11... | collective-permute-start | bytes 172040 | tf_op jit(solution)/shard_map/ppermute | solution.py:44
  4.1 1.6 %copy-start.3 = (s32[2,128]{1,0:T(2,128)S(1)}, s32[2,128]{1,0:T(2,128)}, u32[]{:S(2)}) copy-start(s32[2,128]{1,0:T(2,128)} %flags.1) | copy-start | bytes 3076
  5.7 0.7 %copy-start.2 = (s32[1,8,2]{1,2,0:T(2,128)S(1)}, s32[1,8,2]{1,2,0:T(2,128)}, u32[]{:S(2)}) copy-start(s32[1,8,2]{1,2,0:T(2,128)} %param.7) | copy-start | bytes 196
  5.7 0.7 %copy-start.4 = (s32[1,8,1]{1,2,0:T(1,128)S(1)}, s32[1,8,1]{1,2,0:T(1,128)}, u32[]{:S(2)}) copy-start(s32[1,8,1]{1,2,0:T(1,128)} %param.8) | copy-start | bytes 100
  7.2 13.5 %copy-start.1 = (f32[1,2,512,128]{3,2,1,0:T(8,128)S(1)}, f32[1,2,512,128]{3,2,1,0:T(8,128)}, u32[]{:S(2)}) copy-start(f32[1,2,512,128]{3,2,1,0:T(8,128)} %param.9) | copy-start | bytes 1572868
  7.3 4.4 %collective-permute-start.2 = (bf16[1,4,2,16,128]{4,3,2,1,0:T(8,128)(2,1)S(1)}, bf16[1,4,2,16,128]{4,3,2,1,0:T(8,128)(2,1)S(1)}, u32[]{:S(2)}, u32[]{:S(2)}) collective-permute-start(bf16[1,4,2,16,128]{4,3,2,1,0:T(8,128)(2,1)S(1)} %get-tuple-element.12), channel_id=1, source_target_pairs={{0,4},{4,0},{8,12},{12,8},{16,20},{20,16},{24,28},{28,24},{1,5},{5... | collective-permute-start | bytes 98312 | tf_op jit(solution)/shard_map/ppermute | solution.py:137
  11.7 4.0 %collective-permute-start.3 = (bf16[2,2,2,16,128]{4,3,2,0,1:T(8,128)(2,1)S(1)}, bf16[2,2,2,16,128]{4,3,2,0,1:T(8,128)(2,1)S(1)}, u32[]{:S(2)}, u32[]{:S(2)}) collective-permute-start(bf16[2,2,2,16,128]{4,3,2,0,1:T(8,128)(2,1)S(1)} %bitcast.38), channel_id=1, source_target_pairs={{0,8},{4,12},{8,0},{12,4},{16,24},{20,28},{24,16},{28,20},{1,9},{5... | collective-permute-start | bytes 98312 | tf_op jit(solution)/shard_map/ppermute | solution.py:137
  15.8 5.0 %collective-permute-start.4 = (bf16[4,1,2,16,128]{4,3,2,0,1:T(8,128)(2,1)S(1)}, bf16[4,1,2,16,128]{4,3,2,0,1:T(8,128)(2,1)S(1)}, u32[]{:S(2)}, u32[]{:S(2)}) collective-permute-start(bf16[4,1,2,16,128]{4,3,2,0,1:T(8,128)(2,1)S(1)} %get-tuple-element.8), channel_id=1, source_target_pairs={{0,16},{4,20},{8,24},{12,28},{16,0},{20,4},{24,8},{28,12},{1,17},{... | collective-permute-start | bytes 98312 | tf_op jit(solution)/shard_map/ppermute | solution.py:137

commit v3 on v2

v3 whole, which is shorter than its diff:
```python
import math

import jax
import jax.numpy as jnp
from jax import lax
from jax.experimental import pallas as pl
from jax.experimental.pallas import tpu as pltpu
from jax.sharding import PartitionSpec as P


TILE = 128
MAXOFF = 7
LAGS = 512
CAP = 2
WIDTH = 2
KERNEL_VMEM = 16 * 2**20


STABILITY_FLOOR = 1e-05


def lag_weights(bin_count, band_size, band):
    total_bins = bin_count * band_size
    shape = (LAGS, 2 * total_bins)
    column = lax.broadcasted_iota(jnp.int32, shape, 1)
    lag_shift = lax.broadcasted_iota(jnp.int32, shape, 0) - LAGS // 2
    block, within = column // (2 * bin_count), column % (2 * bin_count)
    part, frequency = within // bin_count, (block ^ band) * bin_count + within % bin_count
    phase_index = jnp.mod(lag_shift * frequency, total_bins)
    angles = phase_index.astype(jnp.float32) * (2.0 * math.pi / total_bins)
    amplitude = 1.0 / math.sqrt(total_bins)
    return jnp.where(part == 0, jnp.cos(angles) * amplitude, -jnp.sin(angles) * amplitude).astype(
        jnp.bfloat16
    )


def halos(bins_first, quarter, quarters):
    length = bins_first.shape[3]
    width = MAXOFF * TILE
    first = lax.slice_in_dim(bins_first, 0, width, axis=3)
    last = lax.slice_in_dim(bins_first, length - width, length, axis=3)
    even = quarter % 2 == 0
    near_pairs = [(i, i ^ 1) for i in range(quarters)]
    far_pairs = [(i, (i + 1 if i % 2 else i - 1) % quarters) for i in range(quarters)]
    near = lax.ppermute(jnp.where(even, last, first), "chan", near_pairs)
    far = lax.ppermute(jnp.where(even, first, last), "chan", far_pairs)
    return near, far


def tile_of(ref, index):
    start = pl.multiple_of(index * TILE, TILE)
    return ref[:, :, :, pl.ds(start, TILE)].astype(jnp.float32)


def level_of(values):
    energy = values[0] * values[0] + values[1] * values[1]
    return jnp.sqrt(jnp.mean(energy, axis=0, keepdims=True) + STABILITY_FLOOR)[None]


def rounded(values):
    return values.astype(jnp.bfloat16).astype(jnp.float32)


def spectrum_of(left, right):
    real = imag = None
    for a, b in zip(left, right):
        re, im = a[0] * b[0] + a[1] * b[1], a[0] * b[1] - a[1] * b[0]
        real, imag = (re, im) if real is None else (real + re, imag + im)
    return jnp.concatenate([real, imag], axis=0).astype(jnp.bfloat16)


def prepare_kernel(pairs, owners, flags, own, info, left, table, held):
    windows = own.shape[0]
    tiles_here = own.shape[3] // TILE
    quarter, band = lax.axis_index("chan"), lax.axis_index("band")
    even = lax.rem(quarter, 2) == 0
    base = quarter * tiles_here
    row = lax.broadcasted_iota(jnp.int32, info.shape, 0)
    lane = lax.broadcasted_iota(jnp.int32, info.shape, 1)

    def clear(o, carry):
        held[o] = 0
        return carry

    lax.fori_loop(0, held.shape[0], clear, 0)
    table[...] = jnp.zeros_like(table)

    def one_pair(p, notes):
        source, target, owner = pairs[0, p], pairs[1, p], owners[0, p]
        here = target - base
        below, above = here < 0, here >= tiles_here
        side = jnp.where(jnp.where(even, above, below), 1, jnp.where(below | above, 2, 0))
        beside = jnp.clip(jnp.where(below, here + MAXOFF, here - tiles_here), 0, MAXOFF - 1)
        rank = held[owner]
        held[owner] = rank + 1
        slot = (owner ^ band) * CAP + rank
        together = 0
        for w in range(windows):
            together = together + flags[w, source] * flags[w, target]
        divisor = jnp.maximum(together, 1).astype(jnp.float32)
        values = tile_of(own, source - base)
        other = tile_of(own, jnp.clip(here, 0, tiles_here - 1))
        lefts, rights = [], []
        for w in range(windows):
            gate = flags[w, source].astype(jnp.float32)
            tile = rounded(values[w] / level_of(values[w]) * gate)
            tile = tile * flags[w, target].astype(jnp.float32) / divisor
            left[p, w] = tile
            lefts.append(tile)
            rights.append(rounded(other[w] / level_of(other[w])))
        spectrum = spectrum_of(lefts, rights)
        table[slot] = jnp.where(side == 0, spectrum, jnp.zeros_like(spectrum))
        for i, value in enumerate((side, beside, slot)):
            notes = jnp.where((row == i) & (lane == p), value, notes)
        return notes

    count = pairs.shape[1]
    info[...] = lax.fori_loop(
        0, count, one_pair, jnp.zeros(info.shape, jnp.int32), unroll=count <= 8
    )


def finish_kernel(info, left, near, far, table, out, notes, sem):
    copy = pltpu.make_async_copy(info, notes, sem)
    copy.start()
    out[...] = table[...]
    copy.wait()

    def one_pair(p, carry):
        side, beside, slot = notes[0, p], notes[1, p], notes[2, p]
        values = jnp.where(side == 1, tile_of(near, beside), tile_of(far, beside))
        windows = values.shape[0]
        rights = [rounded(values[w] / level_of(values[w])) for w in range(windows)]
        spectrum = spectrum_of([left[p, w] for w in range(windows)], rights)
        out[slot] = jnp.where(side == 0, table[slot], spectrum)
        return carry

    count = left.shape[0]
    lax.fori_loop(0, count, one_pair, 0, unroll=count <= 8)


def in_vmem(array):
    return pltpu.with_memory_space_constraint(array, pltpu.VMEM)


SMEM = pl.BlockSpec(memory_space=pltpu.SMEM)
VMEM = pl.BlockSpec(memory_space=pltpu.VMEM)
PARAMS = pltpu.CompilerParams(vmem_limit_bytes=KERNEL_VMEM)


def prepare(bins_first, window_flags, pair_list, owner_ids, band_size):
    windows, _, bins, _ = bins_first.shape
    count = pair_list.shape[1]
    return pl.pallas_call(
        prepare_kernel,
        out_shape=[
            pltpu.VMEM((8, pl.cdiv(count, 128) * 128), jnp.int32),
            pltpu.VMEM((count, windows, 2, bins, TILE), jnp.float32),
            pltpu.VMEM((band_size * CAP, 2 * bins, TILE), jnp.bfloat16),
        ],
        in_specs=[SMEM, SMEM, SMEM, VMEM],
        out_specs=[VMEM, VMEM, VMEM],
        scratch_shapes=[pltpu.SMEM((band_size,), jnp.int32)],
        compiler_params=PARAMS,
        name="prepare",
    )(pair_list, owner_ids, window_flags, in_vmem(bins_first))


def finish(info, left, table, near, far):
    return pl.pallas_call(
        finish_kernel,
        out_shape=pltpu.VMEM(table.shape, table.dtype),
        in_specs=[VMEM] * 5,
        out_specs=VMEM,
        scratch_shapes=[pltpu.SMEM(info.shape, jnp.int32), pltpu.SemaphoreType.DMA],
        compiler_params=PARAMS,
        name="finish",
    )(*map(in_vmem, (info, left, near, far, table)))


def exchange(table, band_size, quarters):
    bits = band_size.bit_length() - 1
    starts = range(0, bits, WIDTH)
    turns = len(starts) - len(starts) % 2 if quarters % 2 == 0 else 0
    held = table[None]
    for stage, low in enumerate(starts):
        ways = 1 << min(WIDTH, bits - low)
        split = held.reshape(held.shape[0], held.shape[1] // ways, ways, *held.shape[2:])
        parts = []
        for way in range(ways):
            flip = (way << low) * quarters + (1 if stage < turns else 0)
            pairs = [(i, i ^ flip) for i in range(band_size * quarters)]
            part = split[:, :, way]
            parts.append(lax.ppermute(part, ("band", "chan"), pairs) if flip else part)
        held = jnp.concatenate(parts, axis=0)
    return held[:, 0]


def stack_kernel(weights, arrived, stacks, out, sums, sems):
    columns = arrived.shape[0] * arrived.shape[2]
    lags = sums.shape[1]
    parts = sems.shape[1]
    rows = lags // parts
    copies = []
    for s in range(arrived.shape[1]):
        spectrum = arrived[:, s].reshape(columns, TILE)
        for part in range(parts):
            here = pl.ds(part * rows, rows)
            added = jnp.dot(weights[here, :], spectrum, preferred_element_type=jnp.float32)
            sums[s, here, :] = stacks[s, here, :] + added
            copy = pltpu.make_async_copy(sums.at[s, here, :], out.at[s, here, :], sems.at[s, part])
            copy.start()
            copies.append(copy)
    for copy in copies:
        copy.wait()


def stack_lags(weights, arrived, stacks):
    return pl.pallas_call(
        stack_kernel,
        out_shape=jax.ShapeDtypeStruct(stacks.shape, stacks.dtype),
        in_specs=[VMEM, VMEM, VMEM],
        out_specs=pl.BlockSpec(memory_space=pl.ANY),
        scratch_shapes=[
            pltpu.VMEM(stacks.shape, stacks.dtype),
            pltpu.SemaphoreType.DMA((stacks.shape[0], 2)),
        ],
        compiler_params=PARAMS,
        name="stack",
    )(in_vmem(weights), in_vmem(arrived), in_vmem(stacks))


def body(spectra, window_flags, pair_tiles, owners, stacks):
    quarter = lax.axis_index("chan")
    band_size, quarters = lax.axis_size("band"), lax.axis_size("chan")
    bins = spectra.shape[3]
    bins_first = jnp.transpose(spectra, (0, 1, 3, 2))
    near, far = halos(bins_first, quarter, quarters)
    info, left, table = prepare(
        bins_first, window_flags, pair_tiles[0].T, owners[0].T, band_size
    )
    table = finish(info, left, table, near, far)
    arrived = exchange(table.reshape(band_size, CAP, 2 * bins, TILE), band_size, quarters)
    weights = lag_weights(bins, band_size, lax.axis_index("band"))
    return stack_lags(weights, arrived, stacks[0])[None]


def solution(mesh):
    in_specs = (
        P(None, None, "chan", "band"),
        P(),
        P("chan", None, None),
        P("chan", None, None),
        P("chan", "band", None, None),
    )
    out_specs = P("chan", "band", None, None)
    return jax.shard_map(body, mesh=mesh, in_specs=in_specs, out_specs=out_specs, check_vma=False)
```

time: 21.9 us -> 21.3 us (0.973)
  starting transfers between devices: 10.9 us -> 9.85 us
  Pallas kernels: 1.85 us -> 2.54 us
  waiting for transfers between devices: 6.03 us -> 5.7 us
    ppermute x1, waiting for transfers between devices: 1.62 us -> 0.08 us  [halos(): far = lax.ppermute(jnp.where(even, first, last), 'chan', far_pairs)]
    ppermute x3 -> x6, waiting for transfers between devices: 4.4 us -> 5.61 us  [exchange(): parts.append(lax.ppermute(part, ('band', 'chan'), pairs) if flip else part)]
    ppermute x3 -> x6, starting transfers between devices: 7.76 us -> 6.7 us  [exchange(): parts.append(lax.ppermute(part, ('band', 'chan'), pairs) if flip else part)]
    pallas_call x1 -> x2, Pallas kernels: 0.86 us -> 1.54 us  [the longest x1 0.83 us: prepare(): pl.pallas_call(prepare_kernel, out_shape=[pltpu.VMEM((8, pl.cdiv(count, 1...]
    unnamed x12 -> x10, local copies, waits for them, and re-layouts: 0.69 us -> 0.68 us
  transfers between devices with their start and end apart: 5 -> 8, of which waited for: 4 -> 5; matrix products, arithmetic and copies ran while one was open for 6% -> 6% of each run, Pallas kernels for 0% -> 4%
where the time goes in v3:
time: 21.3 us; the launch traced here: 21.1 us
  starting transfers between devices  9.85 us (46%)
  waiting for transfers between devices  5.7 us (27%)
  Pallas kernels  2.54 us (12%)
  other arithmetic  2.2 us (10%)
  local copies, waits for them, and re-layouts  0.69 us (3%)
    ppermute x6, starting transfers between devices, exchange(): parts.append(lax.ppermute(part, ('band', 'chan'), pairs) if flip else part)  6.7 us
    ppermute x6, waiting for transfers between devices, exchange(): parts.append(lax.ppermute(part, ('band', 'chan'), pairs) if flip else part)  5.61 us
    ppermute x1, starting transfers between devices, halos(): far = lax.ppermute(jnp.where(even, first, last), 'chan', far_pairs)  2.47 us
    convert_element_type x1, other arithmetic, lag_weights(): jnp.where(part == 0, jnp.cos(angles) * amplitude, -jnp.sin(angles) * ampl...  1.25 us
    pallas_call x1, Pallas kernels, stack_lags(): pl.pallas_call(stack_kernel, out_shape=jax.ShapeDtypeStruct(stacks.shape,...  1 us
    select_n x1, other arithmetic, halos(): far = lax.ppermute(jnp.where(even, first, last), 'chan', far_pairs)  0.91 us
    pallas_call x1, Pallas kernels, prepare(): pl.pallas_call(prepare_kernel, out_shape=[pltpu.VMEM((8, pl.cdiv(count, 1...  0.83 us
    pallas_call x1, Pallas kernels, finish(): pl.pallas_call(finish_kernel, out_shape=pltpu.VMEM(table.shape, table.dty...  0.72 us
  transfers between devices with their start and end apart: 8, of which 5 were waited for; matrix products, arithmetic and copies ran while one was open for 6% of the time, Pallas kernels for 4%

profile of v3, /device:TPU:0, one launch (start us, length us, event | category | flops | bytes accessed | tf_op | source)
XLA Modules:
  0.0 21.1 jit_solution(7348261423589249780)
XLA Ops:
  0.0 0.0 copy-start
  0.0 0.9 %broadcast_select_fusion = (bf16[2,2,8,896]{3,2,1,0:T(8,128)(2,1)S(1)}, bf16[2,2,8,896]{3,2,1,0:T(8,128)(2,1)S(1)}) fusion(pred[]{:T(512)S(6)} %eq.14, bf16[2,2,8,4096]{3,2,1,0:T(8,128)(2,1)} %bitcast.32), kind=kLoop, calls=%fused_computation.24 | loop fusion | flops 57344 | bytes 229377 | tf_op jit(solution)/shard_map/jit(_where)/select_n | solution.py:46
  0.9 2.5 %collective-permute-start.1 = (bf16[2,2,8,896]{3,2,1,0:T(8,128)(2,1)S(1)}, bf16[2,2,8,896]{3,2,1,0:T(8,128)(2,1)S(1)}, u32[]{:S(2)}, u32[]{:S(2)}) collective-permute-start(bf16[2,2,8,896]{3,2,1,0:T(8,128)(2,1)S(1)} %get-tuple-element.11), channel_id=1, source_target_pairs={{0,3},{1,2},{2,1},{3,0},{4,7},{5,6},{6,5},{7,4},{8,11},{9,10},{10,... | collective-permute-start | bytes 172040 | tf_op jit(solution)/shard_map/ppermute | solution.py:46
  3.4 0.7 %collective-permute-start = (bf16[2,2,8,896]{3,2,1,0:T(8,128)(2,1)S(1)}, bf16[2,2,8,896]{3,2,1,0:T(8,128)(2,1)S(1)}, u32[]{:S(2)}, u32[]{:S(2)}) collective-permute-start(bf16[2,2,8,896]{3,2,1,0:T(8,128)(2,1)S(1)} %get-tuple-element.12), channel_id=1, source_target_pairs={{0,1},{1,0},{2,3},{3,2},{4,5},{5,4},{6,7},{7,6},{8,9},{9,8},{10,11... | collective-permute-start | bytes 172040 | tf_op jit(solution)/shard_map/ppermute | solution.py:45
  4.1 0.0 copy-start.3
  4.1 0.0 copy-start.2
  4.1 0.0 copy-start.4
  4.1 0.0 copy-done
  4.1 0.6 %copy-done.3 = s32[2,128]{1,0:T(2,128)S(1)} copy-done((s32[2,128]{1,0:T(2,128)S(1)}, s32[2,128]{1,0:T(2,128)}, u32[]{:S(2)}) %copy-start.3) | copy-done | bytes 1048
  4.7 0.0 copy-done.2
  4.8 0.0 copy-done.4
  4.8 0.8 %prepare.1 = (s32[8,128]{1,0:T(8,128)S(1)}, f32[8,2,2,8,128]{4,3,2,1,0:T(8,128)S(1)}, bf16[16,16,128]{2,1,0:T(8,128)(2,1)S(1)}) custom-call(s32[2,8]{1,0:T(2,128)S(1)} %bitcast.36, s32[1,8]{1,0:T(1,128)S(1)} %bitcast.37, s32[2,128]{1,0:T(2,128)S(1)} %copy-done.3, bf16[2,2,8,4096]{3,2,1,0:T(8,128)(2,1)S(1)} %bitcast.33), custom_call_target="tpu_custom_call" | custom-call | tf_op jit(solution)/shard_map/prepare/pallas_call | solution.py:154
  5.6 0.1 collective-permute-done.1.far
  5.7 0.0 collective-permute-done.near
  5.7 0.0 copy-start.1
  5.7 0.7 %finish.1 = bf16[16,16,128]{2,1,0:T(8,128)(2,1)S(1)} custom-call(s32[8,128]{1,0:T(8,128)S(1)} %get-tuple-element.8.info, f32[8,2,2,8,128]{4,3,2,1,0:T(8,128)S(1)} %get-tuple-element.9.left, bf16[2,2,8,896]{3,2,1,0:T(8,128)(2,1)S(1)} %collective-permute-done.near, bf16[2,2,8,896]{3,2,1,0:T(8,128)(2,1)S(1)} %collective-permute-done.1.far, ...), custom_call_target="tpu_custom_call" | custom-call | tf_op jit(solution)/shard_map/finish/pallas_call | solution.py:170
  6.4 0.3 %collective-permute-start.2 = (bf16[1,2,2,16,128]{4,3,2,0,1:T(8,128)(2,1)S(1)}, bf16[1,2,2,16,128]{4,3,2,0,1:T(8,128)(2,1)S(1)}, u32[]{:S(2)}, u32[]{:S(2)}) collective-permute-start(bf16[1,2,2,16,128]{4,3,2,0,1:T(8,128)(2,1)S(1)} %get-tuple-element.15), channel_id=1, source_target_pairs={{0,1},{1,0},{2,3},{3,2},{4,5},{5,4},{6,7},{7,6},{8,9},{9,8},{10,11... | collective-permute-start | bytes 49160 | tf_op jit(solution)/shard_map/ppermute | solution.py:194
  6.7 2.4 %collective-permute-start.4 = (bf16[1,2,2,16,128]{4,3,2,0,1:T(8,128)(2,1)S(1)}, bf16[1,2,2,16,128]{4,3,2,0,1:T(8,128)(2,1)S(1)}, u32[]{:S(2)}, u32[]{:S(2)}) collective-permute-start(bf16[1,2,2,16,128]{4,3,2,0,1:T(8,128)(2,1)S(1)} %get-tuple-element.16), channel_id=1, source_target_pairs={{0,9},{1,8},{2,11},{3,10},{4,13},{5,12},{6,15},{7,14},{8,1},{9,0},... | collective-permute-start | bytes 49160 | tf_op jit(solution)/shard_map/ppermute | solution.py:194
  9.1 1.2 %collective-permute-start.3 = (bf16[1,2,2,16,128]{4,3,2,0,1:T(8,128)(2,1)S(1)}, bf16[1,2,2,16,128]{4,3,2,0,1:T(8,128)(2,1)S(1)}, u32[]{:S(2)}, u32[]{:S(2)}) collective-permute-start(bf16[1,2,2,16,128]{4,3,2,0,1:T(8,128)(2,1)S(1)} %get-tuple-element.17), channel_id=1, source_target_pairs={{0,5},{1,4},{2,7},{3,6},{4,1},{5,0},{6,3},{7,2},{8,13},{9,12},{10,... | collective-permute-start | bytes 49160 | tf_op jit(solution)/shard_map/ppermute | solution.py:194
  10.4 0.0 collective-permute-start.5
  10.4 0.0 collective-permute-done.2
  10.4 0.2 collective-permute-done.4
  10.6 1.7 %collective-permute-done.3 = bf16[1,2,2,16,128]{4,3,2,0,1:T(8,128)(2,1)S(1)} collective-permute-done((bf16[1,2,2,16,128]{4,3,2,0,1:T(8,128)(2,1)S(1)}, bf16[1,2,2,16,128]{4,3,2,0,1:T(8,128)(2,1)S(1)}, u32[]{:S(2)}, u32[]{:S(2)}) %collective-permute-start.3) | collective-permute-done | bytes 16416 | tf_op jit(solution)/shard_map/ppermute | solution.py:194
  12.3 2.1 %collective-permute-done.5 = bf16[1,2,2,16,128]{4,3,2,0,1:T(8,128)(2,1)S(1)} collective-permute-done((bf16[1,2,2,16,128]{4,3,2,0,1:T(8,128)(2,1)S(1)}, bf16[1,2,2,16,128]{4,3,2,0,1:T(8,128)(2,1)S(1)}, u32[]{:S(2)}, u32[]{:S(2)}) %collective-permute-start.5) | collective-permute-done | bytes 16416 | tf_op jit(solution)/shard_map/ppermute | solution.py:194
  14.5 0.5 %collective-permute-start.6 = (bf16[4,1,2,16,128]{4,3,2,0,1:T(8,128)(2,1)S(1)}, bf16[4,1,2,16,128]{4,3,2,0,1:T(8,128)(2,1)S(1)}, u32[]{:S(2)}, u32[]{:S(2)}) collective-permute-start(bf16[4,1,2,16,128]{4,3,2,0,1:T(8,128)(2,1)S(1)} %get-tuple-element.13), channel_id=1, source_target_pairs={{0,1},{1,0},{2,3},{3,2},{4,5},{5,4},{6,7},{7,6},{8,9},{9,8},{10,11... | collective-permute-start | bytes 98312 | tf_op jit(solution)/shard_map/ppermute | solution.py:194
  14.9 2.3 %collective-permute-start.7 = (bf16[4,1,2,16,128]{4,3,2,0,1:T(8,128)(2,1)S(1)}, bf16[4,1,2,16,128]{4,3,2,0,1:T(8,128)(2,1)S(1)}, u32[]{:S(2)}, u32[]{:S(2)}) collective-permute-start(bf16[4,1,2,16,128]{4,3,2,0,1:T(8,128)(2,1)S(1)} %get-tuple-element.14), channel_id=1, source_target_pairs={{0,17},{1,16},{2,19},{3,18},{4,21},{5,20},{6,23},{7,22},{8,25},{9,... | collective-permute-start | bytes 98312 | tf_op jit(solution)/shard_map/ppermute | solution.py:194
  17.2 1.3 %select_convert_fusion.weights = bf16[512,128]{1,0:T(8,128)(2,1)S(1)} fusion(s32[]{:T(128)S(6)} %axis_index.23, s32[128]{0:T(128)S(1)} %get-tuple-element.21, s32[128]{0:T(128)S(1)} %get-tuple-element.23, s32[512]{0:T(512)S(1)} %iota_add_fusion, s32[128]{0:T(128)S(1)} %get-tuple-element.22, s32[128]{0:T(128)S(1)} %get-tuple-element.24, ...), kind=kLoop, calls=%fused_computation.20 | loop fusion | flops 2883584 | bytes 135428 | tf_op jit(solution)/shard_map/convert_element_type | solution.py:32
  18.5 0.0 collective-permute-done.6
  18.5 1.6 %collective-permute-done.7 = bf16[4,1,2,16,128]{4,3,2,0,1:T(8,128)(2,1)S(1)} collective-permute-done((bf16[4,1,2,16,128]{4,3,2,0,1:T(8,128)(2,1)S(1)}, bf16[4,1,2,16,128]{4,3,2,0,1:T(8,128)(2,1)S(1)}, u32[]{:S(2)}, u32[]{:S(2)}) %collective-permute-start.7) | collective-permute-done | bytes 32800 | tf_op jit(solution)/shard_map/ppermute | solution.py:194
  20.1 0.0 copy-done.1
  20.1 1.0 %stack.1 = f32[2,512,128]{2,1,0:T(8,128)} custom-call(bf16[512,128]{1,0:T(8,128)(2,1)S(1)} %select_convert_fusion.weights, bf16[8,2,16,128]{3,2,1,0:T(8,128)(2,1)S(1)} %maximum_bitcast_fusion.1.arrived, f32[2,512,128]{2,1,0:T(8,128)S(1)} %bitcast.34), custom_call_target="tpu_custom_call" | custom-call | tf_op jit(solution)/shard_map/stack/pallas_call | solution.py:219
  (8 shorter events, 0.1 us)
Async XLA Ops:
  0.0 4.1 %copy-start = (bf16[2,2,4096,8]{2,3,1,0:T(8,128)(2,1)S(1)}, bf16[2,2,4096,8]{2,3,1,0:T(8,128)(2,1)}, u32[]{:S(2)}) copy-start(bf16[2,2,4096,8]{2,3,1,0:T(8,128)(2,1)} %param.5) | copy-start | bytes 786436
  0.9 4.8 %collective-permute-start.1 = (bf16[2,2,8,896]{3,2,1,0:T(8,128)(2,1)S(1)}, bf16[2,2,8,896]{3,2,1,0:T(8,128)(2,1)S(1)}, u32[]{:S(2)}, u32[]{:S(2)}) collective-permute-start(bf16[2,2,8,896]{3,2,1,0:T(8,128)(2,1)S(1)} %get-tuple-element.11), channel_id=1, source_target_pairs={{0,3},{1,2},{2,1},{3,0},{4,7},{5,6},{6,5},{7,4},{8,11},{9,10},{10,... | collective-permute-start | bytes 172040 | tf_op jit(solution)/shard_map/ppermute | solution.py:46
  3.4 2.3 %collective-permute-start = (bf16[2,2,8,896]{3,2,1,0:T(8,128)(2,1)S(1)}, bf16[2,2,8,896]{3,2,1,0:T(8,128)(2,1)S(1)}, u32[]{:S(2)}, u32[]{:S(2)}) collective-permute-start(bf16[2,2,8,896]{3,2,1,0:T(8,128)(2,1)S(1)} %get-tuple-element.12), channel_id=1, source_target_pairs={{0,1},{1,0},{2,3},{3,2},{4,5},{5,4},{6,7},{7,6},{8,9},{9,8},{10,11... | collective-permute-start | bytes 172040 | tf_op jit(solution)/shard_map/ppermute | solution.py:45
  4.1 0.7 %copy-start.3 = (s32[2,128]{1,0:T(2,128)S(1)}, s32[2,128]{1,0:T(2,128)}, u32[]{:S(2)}) copy-start(s32[2,128]{1,0:T(2,128)} %flags.1) | copy-start | bytes 3076
  4.1 0.7 %copy-start.2 = (s32[1,8,2]{1,2,0:T(2,128)S(1)}, s32[1,8,2]{1,2,0:T(2,128)}, u32[]{:S(2)}) copy-start(s32[1,8,2]{1,2,0:T(2,128)} %param.7) | copy-start | bytes 196
  4.1 0.7 %copy-start.4 = (s32[1,8,1]{1,2,0:T(1,128)S(1)}, s32[1,8,1]{1,2,0:T(1,128)}, u32[]{:S(2)}) copy-start(s32[1,8,1]{1,2,0:T(1,128)} %param.8) | copy-start | bytes 100
  5.7 14.4 %copy-start.1 = (f32[1,2,512,128]{3,2,1,0:T(8,128)S(1)}, f32[1,2,512,128]{3,2,1,0:T(8,128)}, u32[]{:S(2)}) copy-start(f32[1,2,512,128]{3,2,1,0:T(8,128)} %param.9) | copy-start | bytes 1572868
  6.4 3.9 %collective-permute-start.2 = (bf16[1,2,2,16,128]{4,3,2,0,1:T(8,128)(2,1)S(1)}, bf16[1,2,2,16,128]{4,3,2,0,1:T(8,128)(2,1)S(1)}, u32[]{:S(2)}, u32[]{:S(2)}) collective-permute-start(bf16[1,2,2,16,128]{4,3,2,0,1:T(8,128)(2,1)S(1)} %get-tuple-element.15), channel_id=1, source_target_pairs={{0,1},{1,0},{2,3},{3,2},{4,5},{5,4},{6,7},{7,6},{8,9},{9,8},{10,11... | collective-permute-start | bytes 49160 | tf_op jit(solution)/shard_map/ppermute | solution.py:194
  6.7 3.8 %collective-permute-start.4 = (bf16[1,2,2,16,128]{4,3,2,0,1:T(8,128)(2,1)S(1)}, bf16[1,2,2,16,128]{4,3,2,0,1:T(8,128)(2,1)S(1)}, u32[]{:S(2)}, u32[]{:S(2)}) collective-permute-start(bf16[1,2,2,16,128]{4,3,2,0,1:T(8,128)(2,1)S(1)} %get-tuple-element.16), channel_id=1, source_target_pairs={{0,9},{1,8},{2,11},{3,10},{4,13},{5,12},{6,15},{7,14},{8,1},{9,0},... | collective-permute-start | bytes 49160 | tf_op jit(solution)/shard_map/ppermute | solution.py:194
  9.1 3.2 %collective-permute-start.3 = (bf16[1,2,2,16,128]{4,3,2,0,1:T(8,128)(2,1)S(1)}, bf16[1,2,2,16,128]{4,3,2,0,1:T(8,128)(2,1)S(1)}, u32[]{:S(2)}, u32[]{:S(2)}) collective-permute-start(bf16[1,2,2,16,128]{4,3,2,0,1:T(8,128)(2,1)S(1)} %get-tuple-element.17), channel_id=1, source_target_pairs={{0,5},{1,4},{2,7},{3,6},{4,1},{5,0},{6,3},{7,2},{8,13},{9,12},{10,... | collective-permute-start | bytes 49160 | tf_op jit(solution)/shard_map/ppermute | solution.py:194
  10.4 4.1 %collective-permute-start.5 = (bf16[1,2,2,16,128]{4,3,2,0,1:T(8,128)(2,1)S(1)}, bf16[1,2,2,16,128]{4,3,2,0,1:T(8,128)(2,1)S(1)}, u32[]{:S(2)}, u32[]{:S(2)}) collective-permute-start(bf16[1,2,2,16,128]{4,3,2,0,1:T(8,128)(2,1)S(1)} %get-tuple-element.18), channel_id=1, source_target_pairs={{0,13},{1,12},{2,15},{3,14},{4,9},{5,8},{6,11},{7,10},{8,5},{9,4},... | collective-permute-start | bytes 49160 | tf_op jit(solution)/shard_map/ppermute | solution.py:194
  14.5 4.0 %collective-permute-start.6 = (bf16[4,1,2,16,128]{4,3,2,0,1:T(8,128)(2,1)S(1)}, bf16[4,1,2,16,128]{4,3,2,0,1:T(8,128)(2,1)S(1)}, u32[]{:S(2)}, u32[]{:S(2)}) collective-permute-start(bf16[4,1,2,16,128]{4,3,2,0,1:T(8,128)(2,1)S(1)} %get-tuple-element.13), channel_id=1, source_target_pairs={{0,1},{1,0},{2,3},{3,2},{4,5},{5,4},{6,7},{7,6},{8,9},{9,8},{10,11... | collective-permute-start | bytes 98312 | tf_op jit(solution)/shard_map/ppermute | solution.py:194
  14.9 5.2 %collective-permute-start.7 = (bf16[4,1,2,16,128]{4,3,2,0,1:T(8,128)(2,1)S(1)}, bf16[4,1,2,16,128]{4,3,2,0,1:T(8,128)(2,1)S(1)}, u32[]{:S(2)}, u32[]{:S(2)}) collective-permute-start(bf16[4,1,2,16,128]{4,3,2,0,1:T(8,128)(2,1)S(1)} %get-tuple-element.14), channel_id=1, source_target_pairs={{0,17},{1,16},{2,19},{3,18},{4,21},{5,20},{6,23},{7,22},{8,25},{9,... | collective-permute-start | bytes 98312 | tf_op jit(solution)/shard_map/ppermute | solution.py:194

commit v4 on v3

--- a/solution.py
+++ b/solution.py
@@ -75,8 +75,6 @@
     quarter, band = lax.axis_index("chan"), lax.axis_index("band")
     even = lax.rem(quarter, 2) == 0
     base = quarter * tiles_here
-    row = lax.broadcasted_iota(jnp.int32, info.shape, 0)
-    lane = lax.broadcasted_iota(jnp.int32, info.shape, 1)
 
     def clear(o, carry):
         held[o] = 0
@@ -85,7 +83,7 @@
     lax.fori_loop(0, held.shape[0], clear, 0)
     table[...] = jnp.zeros_like(table)
 
-    def one_pair(p, notes):
+    def one_pair(p, carry):
         source, target, owner = pairs[0, p], pairs[1, p], owners[0, p]
         here = target - base
         below, above = here < 0, here >= tiles_here
@@ -110,24 +108,19 @@
             rights.append(rounded(other[w] / level_of(other[w])))
         spectrum = spectrum_of(lefts, rights)
         table[slot] = jnp.where(side == 0, spectrum, jnp.zeros_like(spectrum))
-        for i, value in enumerate((side, beside, slot)):
-            notes = jnp.where((row == i) & (lane == p), value, notes)
-        return notes
+        info[p] = jnp.full(info.shape[1:], (slot * MAXOFF + beside) * 3 + side)
+        return carry
 
     count = pairs.shape[1]
-    info[...] = lax.fori_loop(
-        0, count, one_pair, jnp.zeros(info.shape, jnp.int32), unroll=count <= 8
-    )
-
-
-def finish_kernel(info, left, near, far, table, out, notes, sem):
-    copy = pltpu.make_async_copy(info, notes, sem)
-    copy.start()
+    lax.fori_loop(0, count, one_pair, 0, unroll=count <= 8)
+
+
+def finish_kernel(info, left, near, far, table, out):
     out[...] = table[...]
-    copy.wait()
 
     def one_pair(p, carry):
-        side, beside, slot = notes[0, p], notes[1, p], notes[2, p]
+        note = info[p][0, 0]
+        side, beside, slot = note % 3, note // 3 % MAXOFF, note // (3 * MAXOFF)
         values = jnp.where(side == 1, tile_of(near, beside), tile_of(far, beside))
         windows = values.shape[0]
         rights = [rounded(values[w] / level_of(values[w])) for w in range(windows)]
@@ -154,7 +147,7 @@
     return pl.pallas_call(
         prepare_kernel,
         out_shape=[
-            pltpu.VMEM((8, pl.cdiv(count, 128) * 128), jnp.int32),
+            pltpu.VMEM((count, 8, TILE), jnp.int32),
             pltpu.VMEM((count, windows, 2, bins, TILE), jnp.float32),
             pltpu.VMEM((band_size * CAP, 2 * bins, TILE), jnp.bfloat16),
         ],
@@ -172,7 +165,6 @@
         out_shape=pltpu.VMEM(table.shape, table.dtype),
         in_specs=[VMEM] * 5,
         out_specs=VMEM,
-        scratch_shapes=[pltpu.SMEM(info.shape, jnp.int32), pltpu.SemaphoreType.DMA],
         compiler_params=PARAMS,
         name="finish",
     )(*map(in_vmem, (info, left, near, far, table)))

time: 21.3 us -> 20.7 us (0.972)
  Pallas kernels: 2.54 us -> 2.04 us
    pallas_call x1, Pallas kernels: 0.72 us -> 0.21 us  [finish(): pl.pallas_call(finish_kernel, out_shape=pltpu.VMEM(table.shape, table.dty...]
where the time goes in v4:
time: 20.7 us; the launch traced here: 20.6 us
  starting transfers between devices  9.85 us (48%)
  waiting for transfers between devices  5.68 us (27%)
  other arithmetic  2.2 us (11%)
  Pallas kernels  2.04 us (10%)
  local copies, waits for them, and re-layouts  0.69 us (3%)
    ppermute x6, starting transfers between devices, exchange(): parts.append(lax.ppermute(part, ('band', 'chan'), pairs) if flip else part)  6.7 us
    ppermute x6, waiting for transfers between devices, exchange(): parts.append(lax.ppermute(part, ('band', 'chan'), pairs) if flip else part)  5.61 us
    ppermute x1, starting transfers between devices, halos(): far = lax.ppermute(jnp.where(even, first, last), 'chan', far_pairs)  2.47 us
    convert_element_type x1, other arithmetic, lag_weights(): jnp.where(part == 0, jnp.cos(angles) * amplitude, -jnp.sin(angles) * ampl...  1.25 us
    pallas_call x1, Pallas kernels, stack_lags(): pl.pallas_call(stack_kernel, out_shape=jax.ShapeDtypeStruct(stacks.shape,...  1 us
    select_n x1, other arithmetic, halos(): far = lax.ppermute(jnp.where(even, first, last), 'chan', far_pairs)  0.91 us
    pallas_call x1, Pallas kernels, prepare(): pl.pallas_call(prepare_kernel, out_shape=[pltpu.VMEM((count, 8, TILE), jn...  0.84 us
    unnamed x10, local copies, waits for them, and re-layouts  0.68 us
  transfers between devices with their start and end apart: 8, of which 5 were waited for; matrix products, arithmetic and copies ran while one was open for 6% of the time, Pallas kernels for 4%

profile of v4, /device:TPU:0, one launch (start us, length us, event | category | flops | bytes accessed | tf_op | source)
XLA Modules:
  0.0 20.6 jit_solution(10303160117050405135)
XLA Ops:
  0.0 0.0 copy-start
  0.0 0.9 %broadcast_select_fusion = (bf16[2,2,8,896]{3,2,1,0:T(8,128)(2,1)S(1)}, bf16[2,2,8,896]{3,2,1,0:T(8,128)(2,1)S(1)}) fusion(pred[]{:T(512)S(6)} %eq.14, bf16[2,2,8,4096]{3,2,1,0:T(8,128)(2,1)} %bitcast.32), kind=kLoop, calls=%fused_computation.24 | loop fusion | flops 57344 | bytes 229377 | tf_op jit(solution)/shard_map/jit(_where)/select_n | solution.py:46
  0.9 2.5 %collective-permute-start.1 = (bf16[2,2,8,896]{3,2,1,0:T(8,128)(2,1)S(1)}, bf16[2,2,8,896]{3,2,1,0:T(8,128)(2,1)S(1)}, u32[]{:S(2)}, u32[]{:S(2)}) collective-permute-start(bf16[2,2,8,896]{3,2,1,0:T(8,128)(2,1)S(1)} %get-tuple-element.11), channel_id=1, source_target_pairs={{0,3},{1,2},{2,1},{3,0},{4,7},{5,6},{6,5},{7,4},{8,11},{9,10},{10,... | collective-permute-start | bytes 172040 | tf_op jit(solution)/shard_map/ppermute | solution.py:46
  3.4 0.7 %collective-permute-start = (bf16[2,2,8,896]{3,2,1,0:T(8,128)(2,1)S(1)}, bf16[2,2,8,896]{3,2,1,0:T(8,128)(2,1)S(1)}, u32[]{:S(2)}, u32[]{:S(2)}) collective-permute-start(bf16[2,2,8,896]{3,2,1,0:T(8,128)(2,1)S(1)} %get-tuple-element.12), channel_id=1, source_target_pairs={{0,1},{1,0},{2,3},{3,2},{4,5},{5,4},{6,7},{7,6},{8,9},{9,8},{10,11... | collective-permute-start | bytes 172040 | tf_op jit(solution)/shard_map/ppermute | solution.py:45
  4.1 0.0 copy-start.3
  4.1 0.0 copy-start.2
  4.1 0.0 copy-start.4
  4.1 0.0 copy-done
  4.1 0.6 %copy-done.3 = s32[2,128]{1,0:T(2,128)S(1)} copy-done((s32[2,128]{1,0:T(2,128)S(1)}, s32[2,128]{1,0:T(2,128)}, u32[]{:S(2)}) %copy-start.3) | copy-done | bytes 1048
  4.7 0.0 copy-done.2
  4.8 0.0 copy-done.4
  4.8 0.8 %prepare.1 = (s32[8,8,128]{2,1,0:T(8,128)S(1)}, f32[8,2,2,8,128]{4,3,2,1,0:T(8,128)S(1)}, bf16[16,16,128]{2,1,0:T(8,128)(2,1)S(1)}) custom-call(s32[2,8]{1,0:T(2,128)S(1)} %bitcast.36, s32[1,8]{1,0:T(1,128)S(1)} %bitcast.37, s32[2,128]{1,0:T(2,128)S(1)} %copy-done.3, bf16[2,2,8,4096]{3,2,1,0:T(8,128)(2,1)S(1)} %bitcast.33), custom_call_target="tpu_custom_call" | custom-call | tf_op jit(solution)/shard_map/prepare/pallas_call | solution.py:147
  5.6 0.1 collective-permute-done.1.far
  5.7 0.0 collective-permute-done.near
  5.7 0.0 copy-start.1
  5.7 0.2 %finish.1 = bf16[16,16,128]{2,1,0:T(8,128)(2,1)S(1)} custom-call(s32[8,8,128]{2,1,0:T(8,128)S(1)} %get-tuple-element.8.info, f32[8,2,2,8,128]{4,3,2,1,0:T(8,128)S(1)} %get-tuple-element.9.left, bf16[2,2,8,896]{3,2,1,0:T(8,128)(2,1)S(1)} %collective-permute-done.near, bf16[2,2,8,896]{3,2,1,0:T(8,128)(2,1)S(1)} %collective-permute-done.1.far, ...), custom_call_target="tpu_custom_call" | custom-call | tf_op jit(solution)/shard_map/finish/pallas_call | solution.py:163
  5.9 0.3 %collective-permute-start.2 = (bf16[1,2,2,16,128]{4,3,2,0,1:T(8,128)(2,1)S(1)}, bf16[1,2,2,16,128]{4,3,2,0,1:T(8,128)(2,1)S(1)}, u32[]{:S(2)}, u32[]{:S(2)}) collective-permute-start(bf16[1,2,2,16,128]{4,3,2,0,1:T(8,128)(2,1)S(1)} %get-tuple-element.15), channel_id=1, source_target_pairs={{0,1},{1,0},{2,3},{3,2},{4,5},{5,4},{6,7},{7,6},{8,9},{9,8},{10,11... | collective-permute-start | bytes 49160 | tf_op jit(solution)/shard_map/ppermute | solution.py:186
  6.2 2.4 %collective-permute-start.4 = (bf16[1,2,2,16,128]{4,3,2,0,1:T(8,128)(2,1)S(1)}, bf16[1,2,2,16,128]{4,3,2,0,1:T(8,128)(2,1)S(1)}, u32[]{:S(2)}, u32[]{:S(2)}) collective-permute-start(bf16[1,2,2,16,128]{4,3,2,0,1:T(8,128)(2,1)S(1)} %get-tuple-element.16), channel_id=1, source_target_pairs={{0,9},{1,8},{2,11},{3,10},{4,13},{5,12},{6,15},{7,14},{8,1},{9,0},... | collective-permute-start | bytes 49160 | tf_op jit(solution)/shard_map/ppermute | solution.py:186
  8.6 1.2 %collective-permute-start.3 = (bf16[1,2,2,16,128]{4,3,2,0,1:T(8,128)(2,1)S(1)}, bf16[1,2,2,16,128]{4,3,2,0,1:T(8,128)(2,1)S(1)}, u32[]{:S(2)}, u32[]{:S(2)}) collective-permute-start(bf16[1,2,2,16,128]{4,3,2,0,1:T(8,128)(2,1)S(1)} %get-tuple-element.17), channel_id=1, source_target_pairs={{0,5},{1,4},{2,7},{3,6},{4,1},{5,0},{6,3},{7,2},{8,13},{9,12},{10,... | collective-permute-start | bytes 49160 | tf_op jit(solution)/shard_map/ppermute | solution.py:186
  9.9 0.0 collective-permute-start.5
  9.9 0.0 collective-permute-done.2
  9.9 0.2 collective-permute-done.4
  10.1 1.7 %collective-permute-done.3 = bf16[1,2,2,16,128]{4,3,2,0,1:T(8,128)(2,1)S(1)} collective-permute-done((bf16[1,2,2,16,128]{4,3,2,0,1:T(8,128)(2,1)S(1)}, bf16[1,2,2,16,128]{4,3,2,0,1:T(8,128)(2,1)S(1)}, u32[]{:S(2)}, u32[]{:S(2)}) %collective-permute-start.3) | collective-permute-done | bytes 16416 | tf_op jit(solution)/shard_map/ppermute | solution.py:186
  11.8 2.1 %collective-permute-done.5 = bf16[1,2,2,16,128]{4,3,2,0,1:T(8,128)(2,1)S(1)} collective-permute-done((bf16[1,2,2,16,128]{4,3,2,0,1:T(8,128)(2,1)S(1)}, bf16[1,2,2,16,128]{4,3,2,0,1:T(8,128)(2,1)S(1)}, u32[]{:S(2)}, u32[]{:S(2)}) %collective-permute-start.5) | collective-permute-done | bytes 16416 | tf_op jit(solution)/shard_map/ppermute | solution.py:186
  13.9 0.5 %collective-permute-start.6 = (bf16[4,1,2,16,128]{4,3,2,0,1:T(8,128)(2,1)S(1)}, bf16[4,1,2,16,128]{4,3,2,0,1:T(8,128)(2,1)S(1)}, u32[]{:S(2)}, u32[]{:S(2)}) collective-permute-start(bf16[4,1,2,16,128]{4,3,2,0,1:T(8,128)(2,1)S(1)} %get-tuple-element.13), channel_id=1, source_target_pairs={{0,1},{1,0},{2,3},{3,2},{4,5},{5,4},{6,7},{7,6},{8,9},{9,8},{10,11... | collective-permute-start | bytes 98312 | tf_op jit(solution)/shard_map/ppermute | solution.py:186
  14.4 2.3 %collective-permute-start.7 = (bf16[4,1,2,16,128]{4,3,2,0,1:T(8,128)(2,1)S(1)}, bf16[4,1,2,16,128]{4,3,2,0,1:T(8,128)(2,1)S(1)}, u32[]{:S(2)}, u32[]{:S(2)}) collective-permute-start(bf16[4,1,2,16,128]{4,3,2,0,1:T(8,128)(2,1)S(1)} %get-tuple-element.14), channel_id=1, source_target_pairs={{0,17},{1,16},{2,19},{3,18},{4,21},{5,20},{6,23},{7,22},{8,25},{9,... | collective-permute-start | bytes 98312 | tf_op jit(solution)/shard_map/ppermute | solution.py:186
  16.7 1.3 %select_convert_fusion.weights = bf16[512,128]{1,0:T(8,128)(2,1)S(1)} fusion(s32[]{:T(128)S(6)} %axis_index.23, s32[128]{0:T(128)S(1)} %get-tuple-element.21, s32[128]{0:T(128)S(1)} %get-tuple-element.23, s32[512]{0:T(512)S(1)} %iota_add_fusion, s32[128]{0:T(128)S(1)} %get-tuple-element.22, s32[128]{0:T(128)S(1)} %get-tuple-element.24, ...), kind=kLoop, calls=%fused_computation.20 | loop fusion | flops 2883584 | bytes 135428 | tf_op jit(solution)/shard_map/convert_element_type | solution.py:32
  18.0 0.0 collective-permute-done.6
  18.0 1.6 %collective-permute-done.7 = bf16[4,1,2,16,128]{4,3,2,0,1:T(8,128)(2,1)S(1)} collective-permute-done((bf16[4,1,2,16,128]{4,3,2,0,1:T(8,128)(2,1)S(1)}, bf16[4,1,2,16,128]{4,3,2,0,1:T(8,128)(2,1)S(1)}, u32[]{:S(2)}, u32[]{:S(2)}) %collective-permute-start.7) | collective-permute-done | bytes 32800 | tf_op jit(solution)/shard_map/ppermute | solution.py:186
  19.6 0.0 copy-done.1
  19.6 1.0 %stack.1 = f32[2,512,128]{2,1,0:T(8,128)} custom-call(bf16[512,128]{1,0:T(8,128)(2,1)S(1)} %select_convert_fusion.weights, bf16[8,2,16,128]{3,2,1,0:T(8,128)(2,1)S(1)} %maximum_bitcast_fusion.1.arrived, f32[2,512,128]{2,1,0:T(8,128)S(1)} %bitcast.34), custom_call_target="tpu_custom_call" | custom-call | tf_op jit(solution)/shard_map/stack/pallas_call | solution.py:211
  (8 shorter events, 0.1 us)
Async XLA Ops:
  0.0 4.1 %copy-start = (bf16[2,2,4096,8]{2,3,1,0:T(8,128)(2,1)S(1)}, bf16[2,2,4096,8]{2,3,1,0:T(8,128)(2,1)}, u32[]{:S(2)}) copy-start(bf16[2,2,4096,8]{2,3,1,0:T(8,128)(2,1)} %param.5) | copy-start | bytes 786436
  0.9 4.8 %collective-permute-start.1 = (bf16[2,2,8,896]{3,2,1,0:T(8,128)(2,1)S(1)}, bf16[2,2,8,896]{3,2,1,0:T(8,128)(2,1)S(1)}, u32[]{:S(2)}, u32[]{:S(2)}) collective-permute-start(bf16[2,2,8,896]{3,2,1,0:T(8,128)(2,1)S(1)} %get-tuple-element.11), channel_id=1, source_target_pairs={{0,3},{1,2},{2,1},{3,0},{4,7},{5,6},{6,5},{7,4},{8,11},{9,10},{10,... | collective-permute-start | bytes 172040 | tf_op jit(solution)/shard_map/ppermute | solution.py:46
  3.4 2.3 %collective-permute-start = (bf16[2,2,8,896]{3,2,1,0:T(8,128)(2,1)S(1)}, bf16[2,2,8,896]{3,2,1,0:T(8,128)(2,1)S(1)}, u32[]{:S(2)}, u32[]{:S(2)}) collective-permute-start(bf16[2,2,8,896]{3,2,1,0:T(8,128)(2,1)S(1)} %get-tuple-element.12), channel_id=1, source_target_pairs={{0,1},{1,0},{2,3},{3,2},{4,5},{5,4},{6,7},{7,6},{8,9},{9,8},{10,11... | collective-permute-start | bytes 172040 | tf_op jit(solution)/shard_map/ppermute | solution.py:45
  4.1 0.7 %copy-start.3 = (s32[2,128]{1,0:T(2,128)S(1)}, s32[2,128]{1,0:T(2,128)}, u32[]{:S(2)}) copy-start(s32[2,128]{1,0:T(2,128)} %flags.1) | copy-start | bytes 3076
  4.1 0.7 %copy-start.2 = (s32[1,8,2]{1,2,0:T(2,128)S(1)}, s32[1,8,2]{1,2,0:T(2,128)}, u32[]{:S(2)}) copy-start(s32[1,8,2]{1,2,0:T(2,128)} %param.7) | copy-start | bytes 196
  4.1 0.7 %copy-start.4 = (s32[1,8,1]{1,2,0:T(1,128)S(1)}, s32[1,8,1]{1,2,0:T(1,128)}, u32[]{:S(2)}) copy-start(s32[1,8,1]{1,2,0:T(1,128)} %param.8) | copy-start | bytes 100
  5.7 13.9 %copy-start.1 = (f32[1,2,512,128]{3,2,1,0:T(8,128)S(1)}, f32[1,2,512,128]{3,2,1,0:T(8,128)}, u32[]{:S(2)}) copy-start(f32[1,2,512,128]{3,2,1,0:T(8,128)} %param.9) | copy-start | bytes 1572868
  5.9 3.9 %collective-permute-start.2 = (bf16[1,2,2,16,128]{4,3,2,0,1:T(8,128)(2,1)S(1)}, bf16[1,2,2,16,128]{4,3,2,0,1:T(8,128)(2,1)S(1)}, u32[]{:S(2)}, u32[]{:S(2)}) collective-permute-start(bf16[1,2,2,16,128]{4,3,2,0,1:T(8,128)(2,1)S(1)} %get-tuple-element.15), channel_id=1, source_target_pairs={{0,1},{1,0},{2,3},{3,2},{4,5},{5,4},{6,7},{7,6},{8,9},{9,8},{10,11... | collective-permute-start | bytes 49160 | tf_op jit(solution)/shard_map/ppermute | solution.py:186
  6.2 3.8 %collective-permute-start.4 = (bf16[1,2,2,16,128]{4,3,2,0,1:T(8,128)(2,1)S(1)}, bf16[1,2,2,16,128]{4,3,2,0,1:T(8,128)(2,1)S(1)}, u32[]{:S(2)}, u32[]{:S(2)}) collective-permute-start(bf16[1,2,2,16,128]{4,3,2,0,1:T(8,128)(2,1)S(1)} %get-tuple-element.16), channel_id=1, source_target_pairs={{0,9},{1,8},{2,11},{3,10},{4,13},{5,12},{6,15},{7,14},{8,1},{9,0},... | collective-permute-start | bytes 49160 | tf_op jit(solution)/shard_map/ppermute | solution.py:186
  8.6 3.2 %collective-permute-start.3 = (bf16[1,2,2,16,128]{4,3,2,0,1:T(8,128)(2,1)S(1)}, bf16[1,2,2,16,128]{4,3,2,0,1:T(8,128)(2,1)S(1)}, u32[]{:S(2)}, u32[]{:S(2)}) collective-permute-start(bf16[1,2,2,16,128]{4,3,2,0,1:T(8,128)(2,1)S(1)} %get-tuple-element.17), channel_id=1, source_target_pairs={{0,5},{1,4},{2,7},{3,6},{4,1},{5,0},{6,3},{7,2},{8,13},{9,12},{10,... | collective-permute-start | bytes 49160 | tf_op jit(solution)/shard_map/ppermute | solution.py:186
  9.9 4.1 %collective-permute-start.5 = (bf16[1,2,2,16,128]{4,3,2,0,1:T(8,128)(2,1)S(1)}, bf16[1,2,2,16,128]{4,3,2,0,1:T(8,128)(2,1)S(1)}, u32[]{:S(2)}, u32[]{:S(2)}) collective-permute-start(bf16[1,2,2,16,128]{4,3,2,0,1:T(8,128)(2,1)S(1)} %get-tuple-element.18), channel_id=1, source_target_pairs={{0,13},{1,12},{2,15},{3,14},{4,9},{5,8},{6,11},{7,10},{8,5},{9,4},... | collective-permute-start | bytes 49160 | tf_op jit(solution)/shard_map/ppermute | solution.py:186
  13.9 4.0 %collective-permute-start.6 = (bf16[4,1,2,16,128]{4,3,2,0,1:T(8,128)(2,1)S(1)}, bf16[4,1,2,16,128]{4,3,2,0,1:T(8,128)(2,1)S(1)}, u32[]{:S(2)}, u32[]{:S(2)}) collective-permute-start(bf16[4,1,2,16,128]{4,3,2,0,1:T(8,128)(2,1)S(1)} %get-tuple-element.13), channel_id=1, source_target_pairs={{0,1},{1,0},{2,3},{3,2},{4,5},{5,4},{6,7},{7,6},{8,9},{9,8},{10,11... | collective-permute-start | bytes 98312 | tf_op jit(solution)/shard_map/ppermute | solution.py:186
  14.4 5.2 %collective-permute-start.7 = (bf16[4,1,2,16,128]{4,3,2,0,1:T(8,128)(2,1)S(1)}, bf16[4,1,2,16,128]{4,3,2,0,1:T(8,128)(2,1)S(1)}, u32[]{:S(2)}, u32[]{:S(2)}) collective-permute-start(bf16[4,1,2,16,128]{4,3,2,0,1:T(8,128)(2,1)S(1)} %get-tuple-element.14), channel_id=1, source_target_pairs={{0,17},{1,16},{2,19},{3,18},{4,21},{5,20},{6,23},{7,22},{8,25},{9,... | collective-permute-start | bytes 98312 | tf_op jit(solution)/shard_map/ppermute | solution.py:186

commit v5 on v4

--- a/solution.py
+++ b/solution.py
@@ -12,7 +12,6 @@
 MAXOFF = 7
 LAGS = 512
 CAP = 2
-WIDTH = 2
 KERNEL_VMEM = 16 * 2**20
 
 
@@ -132,6 +131,10 @@
     lax.fori_loop(0, count, one_pair, 0, unroll=count <= 8)
 
 
+def in_hbm(array):
+    return pltpu.with_memory_space_constraint(array, pltpu.HBM)
+
+
 def in_vmem(array):
     return pltpu.with_memory_space_constraint(array, pltpu.VMEM)
 
@@ -156,7 +159,7 @@
         scratch_shapes=[pltpu.SMEM((band_size,), jnp.int32)],
         compiler_params=PARAMS,
         name="prepare",
-    )(pair_list, owner_ids, window_flags, in_vmem(bins_first))
+    )(*map(in_hbm, (pair_list, owner_ids, window_flags)), in_vmem(bins_first))
 
 
 def finish(info, left, table, near, far):
@@ -170,21 +173,30 @@
     )(*map(in_vmem, (info, left, near, far, table)))
 
 
+def stages_of(band_size):
+    bits = band_size.bit_length() - 1
+    lows = range(bits - 2, -1, -2) if bits % 2 == 0 else (bits - 1, *range(bits - 3, -1, -2))
+    return [(low, 1 if low == bits - 1 else 2) for low in lows]
+
+
+def turns_of(stages, quarters):
+    return len(stages) - len(stages) % 2 if quarters % 2 == 0 else 0
+
+
 def exchange(table, band_size, quarters):
-    bits = band_size.bit_length() - 1
-    starts = range(0, bits, WIDTH)
-    turns = len(starts) - len(starts) % 2 if quarters % 2 == 0 else 0
+    stages = stages_of(band_size)
+    turns = turns_of(stages, quarters)
     held = table[None]
-    for stage, low in enumerate(starts):
-        ways = 1 << min(WIDTH, bits - low)
-        split = held.reshape(held.shape[0], held.shape[1] // ways, ways, *held.shape[2:])
+    for stage, (low, width) in enumerate(stages):
+        ways = 1 << width
+        split = held.reshape(held.shape[0], ways, 1 << low, *held.shape[2:])
         parts = []
         for way in range(ways):
             flip = (way << low) * quarters + (1 if stage < turns else 0)
             pairs = [(i, i ^ flip) for i in range(band_size * quarters)]
-            part = split[:, :, way]
+            part = split[:, way]
             parts.append(lax.ppermute(part, ("band", "chan"), pairs) if flip else part)
-        held = jnp.concatenate(parts, axis=0)
+        held = jnp.stack(parts, axis=1).reshape(held.shape[0] * ways, 1 << low, *held.shape[2:])
     return held[:, 0]
 
 

time: 20.7 us -> 18.8 us (0.908)
  waiting for transfers between devices: 5.68 us -> 3.92 us
  local copies, waits for them, and re-layouts: 0.69 us -> 0.02 us
  starting transfers between devices: 9.85 us -> 10.2 us
    ppermute x6, waiting for transfers between devices: 5.61 us -> 3.3 us  [exchange(): parts.append(lax.ppermute(part, ('band', 'chan'), pairs) if flip else part)]
    unnamed x10 -> x4, local copies, waits for them, and re-layouts: 0.68 us -> 0.01 us
    ppermute x1, waiting for transfers between devices: 0.07 us -> 0.61 us  [halos(): far = lax.ppermute(jnp.where(even, first, last), 'chan', far_pairs)]
    ppermute x6, starting transfers between devices: 6.7 us -> 7.09 us  [exchange(): parts.append(lax.ppermute(part, ('band', 'chan'), pairs) if flip else part)]
  transfers between devices with their start and end apart: 8 -> 8, of which waited for: 5 -> 4; matrix products, arithmetic and copies ran while one was open for 6% -> 7% of each run, Pallas kernels for 4% -> 5%
where the time goes in v5:
time: 18.8 us; the launch traced here: 18.6 us
  starting transfers between devices  10.2 us (54%)
  waiting for transfers between devices  3.92 us (21%)
  other arithmetic  2.2 us (12%)
  Pallas kernels  2.19 us (12%)
    ppermute x6, starting transfers between devices, exchange(): parts.append(lax.ppermute(part, ('band', 'chan'), pairs) if flip else part)  7.09 us
    ppermute x6, waiting for transfers between devices, exchange(): parts.append(lax.ppermute(part, ('band', 'chan'), pairs) if flip else part)  3.3 us
    ppermute x1, starting transfers between devices, halos(): far = lax.ppermute(jnp.where(even, first, last), 'chan', far_pairs)  2.47 us
    convert_element_type x1, other arithmetic, lag_weights(): jnp.where(part == 0, jnp.cos(angles) * amplitude, -jnp.sin(angles) * ampl...  1.25 us
    pallas_call x1, Pallas kernels, stack_lags(): pl.pallas_call(stack_kernel, out_shape=jax.ShapeDtypeStruct(stacks.shape,...  1 us
    pallas_call x1, Pallas kernels, prepare(): pl.pallas_call(prepare_kernel, out_shape=[pltpu.VMEM((count, 8, TILE), jn...  0.99 us
    select_n x1, other arithmetic, halos(): far = lax.ppermute(jnp.where(even, first, last), 'chan', far_pairs)  0.91 us
    ppermute x1, starting transfers between devices, halos(): near = lax.ppermute(jnp.where(even, last, first), 'chan', near_pairs)  0.68 us
  transfers between devices with their start and end apart: 8, of which 4 were waited for; matrix products, arithmetic and copies ran while one was open for 7% of the time, Pallas kernels for 5%

profile of v5, /device:TPU:0, one launch (start us, length us, event | category | flops | bytes accessed | tf_op | source)
XLA Modules:
  0.0 18.6 jit_solution(17715157391549015760)
XLA Ops:
  0.0 0.0 copy-start
  0.0 0.9 %broadcast_select_fusion = (bf16[2,2,8,896]{3,2,1,0:T(8,128)(2,1)S(1)}, bf16[2,2,8,896]{3,2,1,0:T(8,128)(2,1)S(1)}) fusion(pred[]{:T(512)S(6)} %eq.14, bf16[2,2,8,4096]{3,2,1,0:T(8,128)(2,1)} %bitcast.37), kind=kLoop, calls=%fused_computation.24 | loop fusion | flops 57344 | bytes 229377 | tf_op jit(solution)/shard_map/jit(_where)/select_n | solution.py:45
  0.9 2.5 %collective-permute-start.1 = (bf16[2,2,8,896]{3,2,1,0:T(8,128)(2,1)S(1)}, bf16[2,2,8,896]{3,2,1,0:T(8,128)(2,1)S(1)}, u32[]{:S(2)}, u32[]{:S(2)}) collective-permute-start(bf16[2,2,8,896]{3,2,1,0:T(8,128)(2,1)S(1)} %get-tuple-element.11), channel_id=1, source_target_pairs={{0,3},{1,2},{2,1},{3,0},{4,7},{5,6},{6,5},{7,4},{8,11},{9,10},{10,... | collective-permute-start | bytes 172040 | tf_op jit(solution)/shard_map/ppermute | solution.py:45
  3.4 0.7 %collective-permute-start = (bf16[2,2,8,896]{3,2,1,0:T(8,128)(2,1)S(1)}, bf16[2,2,8,896]{3,2,1,0:T(8,128)(2,1)S(1)}, u32[]{:S(2)}, u32[]{:S(2)}) collective-permute-start(bf16[2,2,8,896]{3,2,1,0:T(8,128)(2,1)S(1)} %get-tuple-element.12), channel_id=1, source_target_pairs={{0,1},{1,0},{2,3},{3,2},{4,5},{5,4},{6,7},{7,6},{8,9},{9,8},{10,11... | collective-permute-start | bytes 172040 | tf_op jit(solution)/shard_map/ppermute | solution.py:44
  4.1 0.0 copy-done
  4.1 1.0 %prepare.1 = (s32[8,8,128]{2,1,0:T(8,128)S(1)}, f32[8,2,2,8,128]{4,3,2,1,0:T(8,128)S(1)}, bf16[16,16,128]{2,1,0:T(8,128)(2,1)S(1)}) custom-call(s32[2,8]{1,0:T(2,128)} %bitcast.48, s32[1,8]{1,0:T(1,128)} %bitcast.49, s32[2,128]{1,0:T(2,128)} %flags.1, bf16[2,2,8,4096]{3,2,1,0:T(8,128)(2,1)S(1)} %bitcast.38), custom_call_target="tpu_custom_call" | custom-call | tf_op jit(solution)/shard_map/prepare/pallas_call | solution.py:150
  5.1 0.6 %collective-permute-done.1.far = bf16[2,2,8,896]{3,2,1,0:T(8,128)(2,1)S(1)} collective-permute-done((bf16[2,2,8,896]{3,2,1,0:T(8,128)(2,1)S(1)}, bf16[2,2,8,896]{3,2,1,0:T(8,128)(2,1)S(1)}, u32[]{:S(2)}, u32[]{:S(2)}) %collective-permute-start.1) | collective-permute-done | bytes 57376 | tf_op jit(solution)/shard_map/ppermute | solution.py:45
  5.7 0.0 collective-permute-done.near
  5.7 0.0 copy-start.1
  5.7 0.2 %finish.1 = bf16[16,16,128]{2,1,0:T(8,128)(2,1)S(1)} custom-call(s32[8,8,128]{2,1,0:T(8,128)S(1)} %get-tuple-element.8.info, f32[8,2,2,8,128]{4,3,2,1,0:T(8,128)S(1)} %get-tuple-element.9.left, bf16[2,2,8,896]{3,2,1,0:T(8,128)(2,1)S(1)} %collective-permute-done.near, bf16[2,2,8,896]{3,2,1,0:T(8,128)(2,1)S(1)} %collective-permute-done.1.far, ...), custom_call_target="tpu_custom_call" | custom-call | tf_op jit(solution)/shard_map/finish/pallas_call | solution.py:166
  5.9 0.3 %collective-permute-start.2 = (bf16[1,4,2,16,128]{4,3,2,1,0:T(8,128)(2,1)S(1)}, bf16[1,4,2,16,128]{4,3,2,1,0:T(8,128)(2,1)S(1)}, u32[]{:S(2)}, u32[]{:S(2)}) collective-permute-start(bf16[1,4,2,16,128]{4,3,2,1,0:T(8,128)(2,1)S(1)} %get-tuple-element.17), channel_id=1, source_target_pairs={{0,1},{1,0},{2,3},{3,2},{4,5},{5,4},{6,7},{7,6},{8,9},{9,8},{10,11... | collective-permute-start | bytes 98312 | tf_op jit(solution)/shard_map/ppermute | solution.py:198
  6.2 3.4 %collective-permute-start.3 = (bf16[1,4,2,16,128]{4,3,2,1,0:T(8,128)(2,1)S(1)}, bf16[1,4,2,16,128]{4,3,2,1,0:T(8,128)(2,1)S(1)}, u32[]{:S(2)}, u32[]{:S(2)}) collective-permute-start(bf16[1,4,2,16,128]{4,3,2,1,0:T(8,128)(2,1)S(1)} %get-tuple-element.18), channel_id=1, source_target_pairs={{0,17},{1,16},{2,19},{3,18},{4,21},{5,20},{6,23},{7,22},{8,25},{9,... | collective-permute-start | bytes 98312 | tf_op jit(solution)/shard_map/ppermute | solution.py:198
  9.6 0.0 collective-permute-done.2
  9.6 1.6 %collective-permute-done.3 = bf16[1,4,2,16,128]{4,3,2,1,0:T(8,128)(2,1)S(1)} collective-permute-done((bf16[1,4,2,16,128]{4,3,2,1,0:T(8,128)(2,1)S(1)}, bf16[1,4,2,16,128]{4,3,2,1,0:T(8,128)(2,1)S(1)}, u32[]{:S(2)}, u32[]{:S(2)}) %collective-permute-start.3) | collective-permute-done | bytes 32800 | tf_op jit(solution)/shard_map/ppermute | solution.py:198
  11.3 0.2 collective-permute-start.4
  11.5 2.7 %collective-permute-start.7 = (bf16[2,1,2,16,128]{4,3,2,0,1:T(8,128)(2,1)S(1)}, bf16[2,1,2,16,128]{4,3,2,0,1:T(8,128)(2,1)S(1)}, u32[]{:S(2)}, u32[]{:S(2)}) collective-permute-start(bf16[2,1,2,16,128]{4,3,2,0,1:T(8,128)(2,1)S(1)} %get-tuple-element.14), channel_id=1, source_target_pairs={{0,13},{1,12},{2,15},{3,14},{4,9},{5,8},{6,11},{7,10},{8,5},{9,4},... | collective-permute-start | bytes 49160 | tf_op jit(solution)/shard_map/ppermute | solution.py:198
  14.2 0.3 %collective-permute-start.6 = (bf16[2,1,2,16,128]{4,3,2,0,1:T(8,128)(2,1)S(1)}, bf16[2,1,2,16,128]{4,3,2,0,1:T(8,128)(2,1)S(1)}, u32[]{:S(2)}, u32[]{:S(2)}) collective-permute-start(bf16[2,1,2,16,128]{4,3,2,0,1:T(8,128)(2,1)S(1)} %get-tuple-element.15), channel_id=1, source_target_pairs={{0,9},{1,8},{2,11},{3,10},{4,13},{5,12},{6,15},{7,14},{8,1},{9,0},... | collective-permute-start | bytes 49160 | tf_op jit(solution)/shard_map/ppermute | solution.py:198
  14.5 0.2 %collective-permute-start.5 = (bf16[2,1,2,16,128]{4,3,2,0,1:T(8,128)(2,1)S(1)}, bf16[2,1,2,16,128]{4,3,2,0,1:T(8,128)(2,1)S(1)}, u32[]{:S(2)}, u32[]{:S(2)}) collective-permute-start(bf16[2,1,2,16,128]{4,3,2,0,1:T(8,128)(2,1)S(1)} %get-tuple-element.16), channel_id=1, source_target_pairs={{0,5},{1,4},{2,7},{3,6},{4,1},{5,0},{6,3},{7,2},{8,13},{9,12},{10,... | collective-permute-start | bytes 49160 | tf_op jit(solution)/shard_map/ppermute | solution.py:198
  14.7 1.3 %select_convert_fusion.weights = bf16[512,128]{1,0:T(8,128)(2,1)S(1)} fusion(s32[]{:T(128)S(6)} %axis_index.23, s32[128]{0:T(128)S(1)} %get-tuple-element.21, s32[128]{0:T(128)S(1)} %get-tuple-element.23, s32[512]{0:T(512)S(1)} %iota_add_fusion, s32[128]{0:T(128)S(1)} %get-tuple-element.22, s32[128]{0:T(128)S(1)} %get-tuple-element.24, ...), kind=kLoop, calls=%fused_computation.20 | loop fusion | flops 2883584 | bytes 135428 | tf_op jit(solution)/shard_map/convert_element_type | solution.py:31
  16.0 0.0 collective-permute-done.4
  16.0 0.0 collective-permute-done.7
  16.0 1.4 %collective-permute-done.6 = bf16[2,1,2,16,128]{4,3,2,0,1:T(8,128)(2,1)S(1)} collective-permute-done((bf16[2,1,2,16,128]{4,3,2,0,1:T(8,128)(2,1)S(1)}, bf16[2,1,2,16,128]{4,3,2,0,1:T(8,128)(2,1)S(1)}, u32[]{:S(2)}, u32[]{:S(2)}) %collective-permute-start.6) | collective-permute-done | bytes 16416 | tf_op jit(solution)/shard_map/ppermute | solution.py:198
  17.4 0.3 %collective-permute-done.5 = bf16[2,1,2,16,128]{4,3,2,0,1:T(8,128)(2,1)S(1)} collective-permute-done((bf16[2,1,2,16,128]{4,3,2,0,1:T(8,128)(2,1)S(1)}, bf16[2,1,2,16,128]{4,3,2,0,1:T(8,128)(2,1)S(1)}, u32[]{:S(2)}, u32[]{:S(2)}) %collective-permute-start.5) | collective-permute-done | bytes 16416 | tf_op jit(solution)/shard_map/ppermute | solution.py:198
  17.6 0.0 copy-done.1
  17.7 1.0 %stack.33 = f32[2,512,128]{2,1,0:T(8,128)} custom-call(bf16[512,128]{1,0:T(8,128)(2,1)S(1)} %select_convert_fusion.weights, bf16[8,2,16,128]{3,2,1,0:T(8,128)(2,1)S(1)} %bitcast.41, f32[2,512,128]{2,1,0:T(8,128)S(1)} %bitcast.39), custom_call_target="tpu_custom_call" | custom-call | tf_op jit(solution)/shard_map/stack/pallas_call | solution.py:223
  (8 shorter events, 0.1 us)
Async XLA Ops:
  0.0 4.1 %copy-start = (bf16[2,2,4096,8]{2,3,1,0:T(8,128)(2,1)S(1)}, bf16[2,2,4096,8]{2,3,1,0:T(8,128)(2,1)}, u32[]{:S(2)}) copy-start(bf16[2,2,4096,8]{2,3,1,0:T(8,128)(2,1)} %param.5) | copy-start | bytes 786436
  0.9 4.8 %collective-permute-start.1 = (bf16[2,2,8,896]{3,2,1,0:T(8,128)(2,1)S(1)}, bf16[2,2,8,896]{3,2,1,0:T(8,128)(2,1)S(1)}, u32[]{:S(2)}, u32[]{:S(2)}) collective-permute-start(bf16[2,2,8,896]{3,2,1,0:T(8,128)(2,1)S(1)} %get-tuple-element.11), channel_id=1, source_target_pairs={{0,3},{1,2},{2,1},{3,0},{4,7},{5,6},{6,5},{7,4},{8,11},{9,10},{10,... | collective-permute-start | bytes 172040 | tf_op jit(solution)/shard_map/ppermute | solution.py:45
  3.4 2.3 %collective-permute-start = (bf16[2,2,8,896]{3,2,1,0:T(8,128)(2,1)S(1)}, bf16[2,2,8,896]{3,2,1,0:T(8,128)(2,1)S(1)}, u32[]{:S(2)}, u32[]{:S(2)}) collective-permute-start(bf16[2,2,8,896]{3,2,1,0:T(8,128)(2,1)S(1)} %get-tuple-element.12), channel_id=1, source_target_pairs={{0,1},{1,0},{2,3},{3,2},{4,5},{5,4},{6,7},{7,6},{8,9},{9,8},{10,11... | collective-permute-start | bytes 172040 | tf_op jit(solution)/shard_map/ppermute | solution.py:44
  5.7 11.9 %copy-start.1 = (f32[1,2,512,128]{3,2,1,0:T(8,128)S(1)}, f32[1,2,512,128]{3,2,1,0:T(8,128)}, u32[]{:S(2)}) copy-start(f32[1,2,512,128]{3,2,1,0:T(8,128)} %param.9) | copy-start | bytes 1572868
  5.9 3.7 %collective-permute-start.2 = (bf16[1,4,2,16,128]{4,3,2,1,0:T(8,128)(2,1)S(1)}, bf16[1,4,2,16,128]{4,3,2,1,0:T(8,128)(2,1)S(1)}, u32[]{:S(2)}, u32[]{:S(2)}) collective-permute-start(bf16[1,4,2,16,128]{4,3,2,1,0:T(8,128)(2,1)S(1)} %get-tuple-element.17), channel_id=1, source_target_pairs={{0,1},{1,0},{2,3},{3,2},{4,5},{5,4},{6,7},{7,6},{8,9},{9,8},{10,11... | collective-permute-start | bytes 98312 | tf_op jit(solution)/shard_map/ppermute | solution.py:198
  6.2 5.1 %collective-permute-start.3 = (bf16[1,4,2,16,128]{4,3,2,1,0:T(8,128)(2,1)S(1)}, bf16[1,4,2,16,128]{4,3,2,1,0:T(8,128)(2,1)S(1)}, u32[]{:S(2)}, u32[]{:S(2)}) collective-permute-start(bf16[1,4,2,16,128]{4,3,2,1,0:T(8,128)(2,1)S(1)} %get-tuple-element.18), channel_id=1, source_target_pairs={{0,17},{1,16},{2,19},{3,18},{4,21},{5,20},{6,23},{7,22},{8,25},{9,... | collective-permute-start | bytes 98312 | tf_op jit(solution)/shard_map/ppermute | solution.py:198
  11.3 4.7 %collective-permute-start.4 = (bf16[2,1,2,16,128]{4,3,2,0,1:T(8,128)(2,1)S(1)}, bf16[2,1,2,16,128]{4,3,2,0,1:T(8,128)(2,1)S(1)}, u32[]{:S(2)}, u32[]{:S(2)}) collective-permute-start(bf16[2,1,2,16,128]{4,3,2,0,1:T(8,128)(2,1)S(1)} %get-tuple-element.13), channel_id=1, source_target_pairs={{0,1},{1,0},{2,3},{3,2},{4,5},{5,4},{6,7},{7,6},{8,9},{9,8},{10,11... | collective-permute-start | bytes 49160 | tf_op jit(solution)/shard_map/ppermute | solution.py:198
  11.5 4.5 %collective-permute-start.7 = (bf16[2,1,2,16,128]{4,3,2,0,1:T(8,128)(2,1)S(1)}, bf16[2,1,2,16,128]{4,3,2,0,1:T(8,128)(2,1)S(1)}, u32[]{:S(2)}, u32[]{:S(2)}) collective-permute-start(bf16[2,1,2,16,128]{4,3,2,0,1:T(8,128)(2,1)S(1)} %get-tuple-element.14), channel_id=1, source_target_pairs={{0,13},{1,12},{2,15},{3,14},{4,9},{5,8},{6,11},{7,10},{8,5},{9,4},... | collective-permute-start | bytes 49160 | tf_op jit(solution)/shard_map/ppermute | solution.py:198
  14.2 3.2 %collective-permute-start.6 = (bf16[2,1,2,16,128]{4,3,2,0,1:T(8,128)(2,1)S(1)}, bf16[2,1,2,16,128]{4,3,2,0,1:T(8,128)(2,1)S(1)}, u32[]{:S(2)}, u32[]{:S(2)}) collective-permute-start(bf16[2,1,2,16,128]{4,3,2,0,1:T(8,128)(2,1)S(1)} %get-tuple-element.15), channel_id=1, source_target_pairs={{0,9},{1,8},{2,11},{3,10},{4,13},{5,12},{6,15},{7,14},{8,1},{9,0},... | collective-permute-start | bytes 49160 | tf_op jit(solution)/shard_map/ppermute | solution.py:198
  14.5 3.2 %collective-permute-start.5 = (bf16[2,1,2,16,128]{4,3,2,0,1:T(8,128)(2,1)S(1)}, bf16[2,1,2,16,128]{4,3,2,0,1:T(8,128)(2,1)S(1)}, u32[]{:S(2)}, u32[]{:S(2)}) collective-permute-start(bf16[2,1,2,16,128]{4,3,2,0,1:T(8,128)(2,1)S(1)} %get-tuple-element.16), channel_id=1, source_target_pairs={{0,5},{1,4},{2,7},{3,6},{4,1},{5,0},{6,3},{7,2},{8,13},{9,12},{10,... | collective-permute-start | bytes 49160 | tf_op jit(solution)/shard_map/ppermute | solution.py:198

commit v6 on v5

--- a/solution.py
+++ b/solution.py
@@ -196,18 +196,20 @@
             pairs = [(i, i ^ flip) for i in range(band_size * quarters)]
             part = split[:, way]
             parts.append(lax.ppermute(part, ("band", "chan"), pairs) if flip else part)
-        held = jnp.stack(parts, axis=1).reshape(held.shape[0] * ways, 1 << low, *held.shape[2:])
-    return held[:, 0]
-
-
-def stack_kernel(weights, arrived, stacks, out, sums, sems):
-    columns = arrived.shape[0] * arrived.shape[2]
+        if low:
+            held = jnp.stack(parts, axis=1).reshape(-1, 1 << low, *held.shape[2:])
+    return [part[:, 0] for part in parts]
+
+
+def stack_kernel(weights, stacks, *refs):
+    *arrived, out, sums, sems = refs
+    columns = weights.shape[1]
     lags = sums.shape[1]
     parts = sems.shape[1]
     rows = lags // parts
     copies = []
-    for s in range(arrived.shape[1]):
-        spectrum = arrived[:, s].reshape(columns, TILE)
+    for s in range(stacks.shape[0]):
+        spectrum = jnp.stack([part[:, s] for part in arrived], axis=1).reshape(columns, TILE)
         for part in range(parts):
             here = pl.ds(part * rows, rows)
             added = jnp.dot(weights[here, :], spectrum, preferred_element_type=jnp.float32)
@@ -223,7 +225,7 @@
     return pl.pallas_call(
         stack_kernel,
         out_shape=jax.ShapeDtypeStruct(stacks.shape, stacks.dtype),
-        in_specs=[VMEM, VMEM, VMEM],
+        in_specs=[VMEM] * (2 + len(arrived)),
         out_specs=pl.BlockSpec(memory_space=pl.ANY),
         scratch_shapes=[
             pltpu.VMEM(stacks.shape, stacks.dtype),
@@ -231,7 +233,7 @@
         ],
         compiler_params=PARAMS,
         name="stack",
-    )(in_vmem(weights), in_vmem(arrived), in_vmem(stacks))
+    )(*map(in_vmem, (weights, stacks, *arrived)))
 
 
 def body(spectra, window_flags, pair_tiles, owners, stacks):

time: 18.8 us -> 18.4 us (0.979)
  waiting for transfers between devices: 3.92 us -> 3.53 us
    ppermute x6, waiting for transfers between devices: 3.3 us -> 2.91 us  [exchange(): parts.append(lax.ppermute(part, ('band', 'chan'), pairs) if flip else part)]
where the time goes in v6:
time: 18.4 us; the launch traced here: 18.2 us
  starting transfers between devices  10.2 us (55%)
  waiting for transfers between devices  3.53 us (19%)
  other arithmetic  2.19 us (12%)
  Pallas kernels  2.19 us (12%)
    ppermute x6, starting transfers between devices, exchange(): parts.append(lax.ppermute(part, ('band', 'chan'), pairs) if flip else part)  7.09 us
    ppermute x6, waiting for transfers between devices, exchange(): parts.append(lax.ppermute(part, ('band', 'chan'), pairs) if flip else part)  2.91 us
    ppermute x1, starting transfers between devices, halos(): far = lax.ppermute(jnp.where(even, first, last), 'chan', far_pairs)  2.47 us
    convert_element_type x1, other arithmetic, lag_weights(): jnp.where(part == 0, jnp.cos(angles) * amplitude, -jnp.sin(angles) * ampl...  1.25 us
    pallas_call x1, Pallas kernels, stack_lags(): pl.pallas_call(stack_kernel, out_shape=jax.ShapeDtypeStruct(stacks.shape,...  0.99 us
    pallas_call x1, Pallas kernels, prepare(): pl.pallas_call(prepare_kernel, out_shape=[pltpu.VMEM((count, 8, TILE), jn...  0.99 us
    select_n x1, other arithmetic, halos(): far = lax.ppermute(jnp.where(even, first, last), 'chan', far_pairs)  0.91 us
    ppermute x1, starting transfers between devices, halos(): near = lax.ppermute(jnp.where(even, last, first), 'chan', near_pairs)  0.68 us
  transfers between devices with their start and end apart: 8, of which 4 were waited for; matrix products, arithmetic and copies ran while one was open for 7% of the time, Pallas kernels for 5%

profile of v6, /device:TPU:0, one launch (start us, length us, event | category | flops | bytes accessed | tf_op | source)
XLA Modules:
  0.0 18.2 jit_solution(9498082929104520255)
XLA Ops:
  0.0 0.0 copy-start
  0.0 0.9 %broadcast_select_fusion = (bf16[2,2,8,896]{3,2,1,0:T(8,128)(2,1)S(1)}, bf16[2,2,8,896]{3,2,1,0:T(8,128)(2,1)S(1)}) fusion(pred[]{:T(512)S(6)} %eq.14, bf16[2,2,8,4096]{3,2,1,0:T(8,128)(2,1)} %bitcast.30), kind=kLoop, calls=%fused_computation.23 | loop fusion | flops 57344 | bytes 229377 | tf_op jit(solution)/shard_map/jit(_where)/select_n | solution.py:45
  0.9 2.5 %collective-permute-start.1 = (bf16[2,2,8,896]{3,2,1,0:T(8,128)(2,1)S(1)}, bf16[2,2,8,896]{3,2,1,0:T(8,128)(2,1)S(1)}, u32[]{:S(2)}, u32[]{:S(2)}) collective-permute-start(bf16[2,2,8,896]{3,2,1,0:T(8,128)(2,1)S(1)} %get-tuple-element.11), channel_id=1, source_target_pairs={{0,3},{1,2},{2,1},{3,0},{4,7},{5,6},{6,5},{7,4},{8,11},{9,10},{10,... | collective-permute-start | bytes 172040 | tf_op jit(solution)/shard_map/ppermute | solution.py:45
  3.4 0.7 %collective-permute-start = (bf16[2,2,8,896]{3,2,1,0:T(8,128)(2,1)S(1)}, bf16[2,2,8,896]{3,2,1,0:T(8,128)(2,1)S(1)}, u32[]{:S(2)}, u32[]{:S(2)}) collective-permute-start(bf16[2,2,8,896]{3,2,1,0:T(8,128)(2,1)S(1)} %get-tuple-element.12), channel_id=1, source_target_pairs={{0,1},{1,0},{2,3},{3,2},{4,5},{5,4},{6,7},{7,6},{8,9},{9,8},{10,11... | collective-permute-start | bytes 172040 | tf_op jit(solution)/shard_map/ppermute | solution.py:44
  4.1 0.0 copy-done
  4.1 1.0 %prepare.1 = (s32[8,8,128]{2,1,0:T(8,128)S(1)}, f32[8,2,2,8,128]{4,3,2,1,0:T(8,128)S(1)}, bf16[16,16,128]{2,1,0:T(8,128)(2,1)S(1)}) custom-call(s32[2,8]{1,0:T(2,128)} %bitcast.40, s32[1,8]{1,0:T(1,128)} %bitcast.41, s32[2,128]{1,0:T(2,128)} %flags.1, bf16[2,2,8,4096]{3,2,1,0:T(8,128)(2,1)S(1)} %bitcast.31), custom_call_target="tpu_custom_call" | custom-call | tf_op jit(solution)/shard_map/prepare/pallas_call | solution.py:150
  5.1 0.6 %collective-permute-done.1.far = bf16[2,2,8,896]{3,2,1,0:T(8,128)(2,1)S(1)} collective-permute-done((bf16[2,2,8,896]{3,2,1,0:T(8,128)(2,1)S(1)}, bf16[2,2,8,896]{3,2,1,0:T(8,128)(2,1)S(1)}, u32[]{:S(2)}, u32[]{:S(2)}) %collective-permute-start.1) | collective-permute-done | bytes 57376 | tf_op jit(solution)/shard_map/ppermute | solution.py:45
  5.7 0.0 collective-permute-done.near
  5.7 0.0 copy-start.1
  5.7 0.2 %finish.1 = bf16[16,16,128]{2,1,0:T(8,128)(2,1)S(1)} custom-call(s32[8,8,128]{2,1,0:T(8,128)S(1)} %get-tuple-element.8.info, f32[8,2,2,8,128]{4,3,2,1,0:T(8,128)S(1)} %get-tuple-element.9.left, bf16[2,2,8,896]{3,2,1,0:T(8,128)(2,1)S(1)} %collective-permute-done.near, bf16[2,2,8,896]{3,2,1,0:T(8,128)(2,1)S(1)} %collective-permute-done.1.far, ...), custom_call_target="tpu_custom_call" | custom-call | tf_op jit(solution)/shard_map/finish/pallas_call | solution.py:166
  5.9 0.3 %collective-permute-start.2 = (bf16[1,4,2,16,128]{4,3,2,1,0:T(8,128)(2,1)S(1)}, bf16[1,4,2,16,128]{4,3,2,1,0:T(8,128)(2,1)S(1)}, u32[]{:S(2)}, u32[]{:S(2)}) collective-permute-start(bf16[1,4,2,16,128]{4,3,2,1,0:T(8,128)(2,1)S(1)} %get-tuple-element.17), channel_id=1, source_target_pairs={{0,1},{1,0},{2,3},{3,2},{4,5},{5,4},{6,7},{7,6},{8,9},{9,8},{10,11... | collective-permute-start | bytes 98312 | tf_op jit(solution)/shard_map/ppermute | solution.py:198
  6.2 3.4 %collective-permute-start.3 = (bf16[1,4,2,16,128]{4,3,2,1,0:T(8,128)(2,1)S(1)}, bf16[1,4,2,16,128]{4,3,2,1,0:T(8,128)(2,1)S(1)}, u32[]{:S(2)}, u32[]{:S(2)}) collective-permute-start(bf16[1,4,2,16,128]{4,3,2,1,0:T(8,128)(2,1)S(1)} %get-tuple-element.18), channel_id=1, source_target_pairs={{0,17},{1,16},{2,19},{3,18},{4,21},{5,20},{6,23},{7,22},{8,25},{9,... | collective-permute-start | bytes 98312 | tf_op jit(solution)/shard_map/ppermute | solution.py:198
  9.6 0.0 collective-permute-done.2
  9.6 1.6 %collective-permute-done.3 = bf16[1,4,2,16,128]{4,3,2,1,0:T(8,128)(2,1)S(1)} collective-permute-done((bf16[1,4,2,16,128]{4,3,2,1,0:T(8,128)(2,1)S(1)}, bf16[1,4,2,16,128]{4,3,2,1,0:T(8,128)(2,1)S(1)}, u32[]{:S(2)}, u32[]{:S(2)}) %collective-permute-start.3) | collective-permute-done | bytes 32800 | tf_op jit(solution)/shard_map/ppermute | solution.py:198
  11.3 2.6 %collective-permute-start.7 = (bf16[2,1,2,16,128]{4,3,2,0,1:T(8,128)(2,1)S(1)}, bf16[2,1,2,16,128]{4,3,2,0,1:T(8,128)(2,1)S(1)}, u32[]{:S(2)}, u32[]{:S(2)}) collective-permute-start(bf16[2,1,2,16,128]{4,3,2,0,1:T(8,128)(2,1)S(1)} %get-tuple-element.13), channel_id=1, source_target_pairs={{0,13},{1,12},{2,15},{3,14},{4,9},{5,8},{6,11},{7,10},{8,5},{9,4},... | collective-permute-start | bytes 49160 | tf_op jit(solution)/shard_map/ppermute | solution.py:198
  13.9 0.2 collective-permute-start.6
  14.1 0.4 %collective-permute-start.5 = (bf16[2,1,2,16,128]{4,3,2,0,1:T(8,128)(2,1)S(1)}, bf16[2,1,2,16,128]{4,3,2,0,1:T(8,128)(2,1)S(1)}, u32[]{:S(2)}, u32[]{:S(2)}) collective-permute-start(bf16[2,1,2,16,128]{4,3,2,0,1:T(8,128)(2,1)S(1)} %get-tuple-element.15), channel_id=1, source_target_pairs={{0,5},{1,4},{2,7},{3,6},{4,1},{5,0},{6,3},{7,2},{8,13},{9,12},{10,... | collective-permute-start | bytes 49160 | tf_op jit(solution)/shard_map/ppermute | solution.py:198
  14.4 0.3 %collective-permute-start.4 = (bf16[2,1,2,16,128]{4,3,2,0,1:T(8,128)(2,1)S(1)}, bf16[2,1,2,16,128]{4,3,2,0,1:T(8,128)(2,1)S(1)}, u32[]{:S(2)}, u32[]{:S(2)}) collective-permute-start(bf16[2,1,2,16,128]{4,3,2,0,1:T(8,128)(2,1)S(1)} %get-tuple-element.16), channel_id=1, source_target_pairs={{0,1},{1,0},{2,3},{3,2},{4,5},{5,4},{6,7},{7,6},{8,9},{9,8},{10,11... | collective-permute-start | bytes 49160 | tf_op jit(solution)/shard_map/ppermute | solution.py:198
  14.7 1.3 %select_convert_fusion.weights = bf16[512,128]{1,0:T(8,128)(2,1)S(1)} fusion(s32[]{:T(128)S(6)} %axis_index.23, s32[128]{0:T(128)S(1)} %get-tuple-element.21, s32[128]{0:T(128)S(1)} %get-tuple-element.23, s32[512]{0:T(512)S(1)} %iota_add_fusion, s32[128]{0:T(128)S(1)} %get-tuple-element.22, s32[128]{0:T(128)S(1)} %get-tuple-element.24, ...), kind=kLoop, calls=%fused_computation.20 | loop fusion | flops 2883584 | bytes 135428 | tf_op jit(solution)/shard_map/convert_element_type | solution.py:31
  16.0 0.0 collective-permute-done.7
  16.0 1.1 %collective-permute-done.6 = bf16[2,1,2,16,128]{4,3,2,0,1:T(8,128)(2,1)S(1)} collective-permute-done((bf16[2,1,2,16,128]{4,3,2,0,1:T(8,128)(2,1)S(1)}, bf16[2,1,2,16,128]{4,3,2,0,1:T(8,128)(2,1)S(1)}, u32[]{:S(2)}, u32[]{:S(2)}) %collective-permute-start.6) | collective-permute-done | bytes 16416 | tf_op jit(solution)/shard_map/ppermute | solution.py:198
  17.1 0.2 collective-permute-done.5
  17.2 0.0 collective-permute-done.4
  17.2 0.0 copy-done.1
  17.2 1.0 %stack.13 = f32[2,512,128]{2,1,0:T(8,128)} custom-call(bf16[512,128]{1,0:T(8,128)(2,1)S(1)} %select_convert_fusion.weights, f32[2,512,128]{2,1,0:T(8,128)S(1)} %bitcast.32, bf16[2,2,16,128]{3,2,1,0:T(8,128)(2,1)S(1)} %bitcast.37, bf16[2,2,16,128]{3,2,1,0:T(8,128)(2,1)S(1)} %bitcast.36, bf16[2,2,16,128]{3,2,1,0:T(8,128)(2,1)S(1)} %bitcast.35, ...), custom_call_target="tpu_custom_call" | custom-call | tf_op jit(solution)/shard_map/stack/pallas_call | solution.py:225
  (7 shorter events, 0.0 us)
Async XLA Ops:
  0.0 4.1 %copy-start = (bf16[2,2,4096,8]{2,3,1,0:T(8,128)(2,1)S(1)}, bf16[2,2,4096,8]{2,3,1,0:T(8,128)(2,1)}, u32[]{:S(2)}) copy-start(bf16[2,2,4096,8]{2,3,1,0:T(8,128)(2,1)} %param.5) | copy-start | bytes 786436
  0.9 4.8 %collective-permute-start.1 = (bf16[2,2,8,896]{3,2,1,0:T(8,128)(2,1)S(1)}, bf16[2,2,8,896]{3,2,1,0:T(8,128)(2,1)S(1)}, u32[]{:S(2)}, u32[]{:S(2)}) collective-permute-start(bf16[2,2,8,896]{3,2,1,0:T(8,128)(2,1)S(1)} %get-tuple-element.11), channel_id=1, source_target_pairs={{0,3},{1,2},{2,1},{3,0},{4,7},{5,6},{6,5},{7,4},{8,11},{9,10},{10,... | collective-permute-start | bytes 172040 | tf_op jit(solution)/shard_map/ppermute | solution.py:45
  3.4 2.3 %collective-permute-start = (bf16[2,2,8,896]{3,2,1,0:T(8,128)(2,1)S(1)}, bf16[2,2,8,896]{3,2,1,0:T(8,128)(2,1)S(1)}, u32[]{:S(2)}, u32[]{:S(2)}) collective-permute-start(bf16[2,2,8,896]{3,2,1,0:T(8,128)(2,1)S(1)} %get-tuple-element.12), channel_id=1, source_target_pairs={{0,1},{1,0},{2,3},{3,2},{4,5},{5,4},{6,7},{7,6},{8,9},{9,8},{10,11... | collective-permute-start | bytes 172040 | tf_op jit(solution)/shard_map/ppermute | solution.py:44
  5.7 11.5 %copy-start.1 = (f32[1,2,512,128]{3,2,1,0:T(8,128)S(1)}, f32[1,2,512,128]{3,2,1,0:T(8,128)}, u32[]{:S(2)}) copy-start(f32[1,2,512,128]{3,2,1,0:T(8,128)} %param.9) | copy-start | bytes 1572868
  5.9 3.7 %collective-permute-start.2 = (bf16[1,4,2,16,128]{4,3,2,1,0:T(8,128)(2,1)S(1)}, bf16[1,4,2,16,128]{4,3,2,1,0:T(8,128)(2,1)S(1)}, u32[]{:S(2)}, u32[]{:S(2)}) collective-permute-start(bf16[1,4,2,16,128]{4,3,2,1,0:T(8,128)(2,1)S(1)} %get-tuple-element.17), channel_id=1, source_target_pairs={{0,1},{1,0},{2,3},{3,2},{4,5},{5,4},{6,7},{7,6},{8,9},{9,8},{10,11... | collective-permute-start | bytes 98312 | tf_op jit(solution)/shard_map/ppermute | solution.py:198
  6.2 5.1 %collective-permute-start.3 = (bf16[1,4,2,16,128]{4,3,2,1,0:T(8,128)(2,1)S(1)}, bf16[1,4,2,16,128]{4,3,2,1,0:T(8,128)(2,1)S(1)}, u32[]{:S(2)}, u32[]{:S(2)}) collective-permute-start(bf16[1,4,2,16,128]{4,3,2,1,0:T(8,128)(2,1)S(1)} %get-tuple-element.18), channel_id=1, source_target_pairs={{0,17},{1,16},{2,19},{3,18},{4,21},{5,20},{6,23},{7,22},{8,25},{9,... | collective-permute-start | bytes 98312 | tf_op jit(solution)/shard_map/ppermute | solution.py:198
  11.3 4.7 %collective-permute-start.7 = (bf16[2,1,2,16,128]{4,3,2,0,1:T(8,128)(2,1)S(1)}, bf16[2,1,2,16,128]{4,3,2,0,1:T(8,128)(2,1)S(1)}, u32[]{:S(2)}, u32[]{:S(2)}) collective-permute-start(bf16[2,1,2,16,128]{4,3,2,0,1:T(8,128)(2,1)S(1)} %get-tuple-element.13), channel_id=1, source_target_pairs={{0,13},{1,12},{2,15},{3,14},{4,9},{5,8},{6,11},{7,10},{8,5},{9,4},... | collective-permute-start | bytes 49160 | tf_op jit(solution)/shard_map/ppermute | solution.py:198
  13.9 3.2 %collective-permute-start.6 = (bf16[2,1,2,16,128]{4,3,2,0,1:T(8,128)(2,1)S(1)}, bf16[2,1,2,16,128]{4,3,2,0,1:T(8,128)(2,1)S(1)}, u32[]{:S(2)}, u32[]{:S(2)}) collective-permute-start(bf16[2,1,2,16,128]{4,3,2,0,1:T(8,128)(2,1)S(1)} %get-tuple-element.14), channel_id=1, source_target_pairs={{0,9},{1,8},{2,11},{3,10},{4,13},{5,12},{6,15},{7,14},{8,1},{9,0},... | collective-permute-start | bytes 49160 | tf_op jit(solution)/shard_map/ppermute | solution.py:198
  14.1 3.2 %collective-permute-start.5 = (bf16[2,1,2,16,128]{4,3,2,0,1:T(8,128)(2,1)S(1)}, bf16[2,1,2,16,128]{4,3,2,0,1:T(8,128)(2,1)S(1)}, u32[]{:S(2)}, u32[]{:S(2)}) collective-permute-start(bf16[2,1,2,16,128]{4,3,2,0,1:T(8,128)(2,1)S(1)} %get-tuple-element.15), channel_id=1, source_target_pairs={{0,5},{1,4},{2,7},{3,6},{4,1},{5,0},{6,3},{7,2},{8,13},{9,12},{10,... | collective-permute-start | bytes 49160 | tf_op jit(solution)/shard_map/ppermute | solution.py:198
  14.4 2.8 %collective-permute-start.4 = (bf16[2,1,2,16,128]{4,3,2,0,1:T(8,128)(2,1)S(1)}, bf16[2,1,2,16,128]{4,3,2,0,1:T(8,128)(2,1)S(1)}, u32[]{:S(2)}, u32[]{:S(2)}) collective-permute-start(bf16[2,1,2,16,128]{4,3,2,0,1:T(8,128)(2,1)S(1)} %get-tuple-element.16), channel_id=1, source_target_pairs={{0,1},{1,0},{2,3},{3,2},{4,5},{5,4},{6,7},{7,6},{8,9},{9,8},{10,11... | collective-permute-start | bytes 49160 | tf_op jit(solution)/shard_map/ppermute | solution.py:198
